TPU v7x, 32 devices: a whole 2x2x4 slice. The times are simulated.
32 devices in a mesh: dp: 8 (over y, x, core), tensor: 4 (over z).
Axes of the slice: x: 2, y: 2, z: 4, core: 2. Of those that a mesh axis runs over, the one named last changes fastest.
Arguments:
- inputs: bfloat16 [16384, 768], P(('dp', 'tensor')), may hold values from -6 to 6
- out_grad: bfloat16 [16384, 768], P(('dp', 'tensor')), may hold values from -6 to 6
- seq_lengths: int32 [8, 3], P('dp'), may hold values from 1 to 1024, 2048 in all within a row
- balance: int32 [8, 2048], P('dp'), may hold values from 0 to 2047, each once within a row
- clusters: int32 [8, 12, 2048], P('dp', 'tensor'), may hold values from 0 to 2047, each once within a row
- query_weight: bfloat16 [768, 768], P('dp', 'tensor'), may hold values from -0.21875 to 0.21875
- query_bias: float32 [768], P('tensor'), may hold values from -3 to 3
- key_weight: bfloat16 [768, 768], P('dp', 'tensor'), may hold values from -0.21875 to 0.21875
- value_weight: bfloat16 [768, 768], P('dp', 'tensor'), may hold values from -0.21875 to 0.21875
- value_bias: float32 [768], P('tensor'), may hold values from -3 to 3
- out_weight: bfloat16 [768, 768], P('tensor', 'dp'), may hold values from -0.875 to 0.875
- out_bias: float32 [768], replicated, may hold values from -3 to 3
- norm1_gain: float32 [768], replicated, may hold values from 0.1 to 1.9
- norm1_bias: float32 [768], replicated, may hold values from -3 to 3
- up_weight: bfloat16 [768, 3072], P('dp', 'tensor'), may hold values from -0.21875 to 0.21875
- up_bias: float32 [3072], P('tensor'), may hold values from -3 to 3
- down_weight: bfloat16 [3072, 768], P('tensor', 'dp'), may hold values from -0.109375 to 0.109375
- down_bias: float32 [768], replicated, may hold values from -3 to 3
- norm2_gain: float32 [768], replicated, may hold values from 0.1 to 1.9
- norm2_bias: float32 [768], replicated, may hold values from -3 to 3
Outputs:
- layer_out: bfloat16 [16384, 768], P(('dp', 'tensor'))
- grad_inputs: float32 [16384, 768], P(('dp', 'tensor'))
- grad_query_weight: float32 [768, 768], P('dp', 'tensor')
- grad_query_bias: float32 [768], P('tensor')
- grad_key_weight: float32 [768, 768], P('dp', 'tensor')
- grad_value_weight: float32 [768, 768], P('dp', 'tensor')
- grad_value_bias: float32 [768], P('tensor')
- grad_out_weight: float32 [768, 768], P('tensor', 'dp')
- grad_out_bias: float32 [768], replicated
- grad_norm1_gain: float32 [768], replicated
- grad_norm1_bias: float32 [768], replicated
- grad_up_weight: float32 [768, 3072], P('dp', 'tensor')
- grad_up_bias: float32 [3072], P('tensor')
- grad_down_weight: float32 [3072, 768], P('tensor', 'dp')
- grad_down_bias: float32 [768], replicated
- grad_norm2_gain: float32 [768], replicated
- grad_norm2_bias: float32 [768], replicated
Inputs may be any that keep to these rules, and one draw needn't show every extreme that they name: `seq_lengths`: each group's lengths sum to 2048; the largest in each group is exactly 1024. `balance`: each group's row is a permutation of its 2048 token indices. `clusters`: each head's row of a group is a permutation of the 2048 balanced positions.
All inputs are finite; a program needn't handle non-finite values.
Results may differ from a plain program's by a relative error of at most 0.019.
Values may be sent and summed in bfloat16 or wider, within the bound.
No kernel may reach another device: no remote copies, remote signals or barrier semaphores. Data moves between devices by JAX's collectives and lax.ppermute only.
A program may use at most 128 MiB of HBM per device.

v0:
```python
import jax
import jax.numpy as jnp
from jax import lax
from jax.sharding import PartitionSpec as P

HD = 64
CL = 128


def layer_norm(values_in, gain, shift):
    center = values_in - jnp.mean(values_in, axis=-1, keepdims=True)
    variance = jnp.mean(center * center, axis=-1, keepdims=True)
    return center * lax.rsqrt(variance + 1e-06) * gain + shift


def gelu_tanh(values_in):
    return jax.nn.gelu(values_in, approximate=True)


def product(left, right):
    return jnp.dot(left, right, preferred_element_type=jnp.float32)


def product_nt(left, right):
    return lax.dot_general(
        left, right, (((1,), (1,)), ((), ())), preferred_element_type=jnp.float32
    )


def product_tn(left, right):
    return lax.dot_general(
        left, right, (((0,), (0,)), ((), ())), preferred_element_type=jnp.float32
    )


def to_slots(values_in, slot_order):
    token_count = values_in.shape[0]
    head_count = slot_order.shape[0]
    per_head = values_in.reshape(token_count, head_count, HD).transpose(1, 0, 2)
    picked = jnp.take_along_axis(per_head, slot_order[:, :, None], axis=1)
    return picked.reshape(head_count, token_count // CL, CL, HD)


def to_tokens(slots, token_place):
    head_count = slots.shape[0]
    flat_slots = slots.reshape(head_count, -1, HD)
    placed = jnp.take_along_axis(flat_slots, token_place[:, :, None], axis=1)
    return placed.transpose(1, 0, 2).reshape(flat_slots.shape[1], head_count * HD)


def masked_scores(query_slots, key_slots, segment_slots):
    raw_scores = jnp.einsum(
        "hcqd,hckd->hcqk", query_slots, key_slots, preferred_element_type=jnp.float32
    ) * HD ** (-0.5)
    same_doc = segment_slots[:, :, :, None] == segment_slots[:, :, None, :]
    return jnp.where(same_doc, raw_scores, -1e30)


def local(
    inputs,
    out_grad,
    seq_lengths,
    balance,
    clusters,
    query_weight,
    query_bias,
    key_weight,
    value_weight,
    value_bias,
    out_weight,
    out_bias,
    norm1_gain,
    norm1_bias,
    up_weight,
    up_bias,
    down_weight,
    down_bias,
    norm2_gain,
    norm2_bias,
):
    row_count = inputs.shape[0]
    tensor_size = lax.axis_size("tensor")
    tensor_rank = lax.axis_index("tensor")
    group_rows = row_count * tensor_size
    local_width = query_weight.shape[1]
    local_hidden = up_weight.shape[1]
    query_full, key_full, value_full, out_full, up_rows, down_cols = (
        lax.all_gather(query_weight, "dp", axis=0, tiled=True),
        lax.all_gather(key_weight, "dp", axis=0, tiled=True),
        lax.all_gather(value_weight, "dp", axis=0, tiled=True),
        lax.all_gather(out_weight, "dp", axis=1, tiled=True),
        lax.all_gather(up_weight, "dp", axis=0, tiled=True),
        lax.all_gather(down_weight, "dp", axis=1, tiled=True),
    )
    positions = jnp.arange(group_rows, dtype=jnp.int32)
    bounds = jnp.cumsum(seq_lengths[0])
    segment = jnp.sum((positions[:, None] >= bounds[None, :]).astype(jnp.int32), axis=1)
    slot_order = jnp.take(balance[0], clusters[0], axis=0)
    token_place = jax.vmap(
        lambda row_order: jnp.zeros((group_rows,), jnp.int32).at[row_order].set(positions)
    )(slot_order)
    segment_slots = jnp.take(segment, slot_order, axis=0).reshape(
        slot_order.shape[0], group_rows // CL, CL
    )
    inputs_all = lax.all_gather(inputs, "tensor", axis=0, tiled=True)
    query_rows = (product(inputs_all, query_full) + query_bias).astype(jnp.bfloat16)
    key_rows = product(inputs_all, key_full).astype(jnp.bfloat16)
    value_rows = (product(inputs_all, value_full) + value_bias).astype(jnp.bfloat16)
    query_slots = to_slots(query_rows, slot_order)
    key_slots = to_slots(key_rows, slot_order)
    value_slots = to_slots(value_rows, slot_order)
    scores = masked_scores(query_slots, key_slots, segment_slots)
    top_score = jnp.max(scores, axis=-1, keepdims=True)
    log_total = top_score + jnp.log(jnp.sum(jnp.exp(scores - top_score), axis=-1, keepdims=True))
    prob_low = jnp.exp(scores - log_total).astype(jnp.bfloat16)
    context_slots = jnp.einsum(
        "hcqk,hckd->hcqd", prob_low, value_slots, preferred_element_type=jnp.float32
    ).astype(jnp.bfloat16)
    context = to_tokens(context_slots, token_place)
    attention = lax.psum_scatter(
        product(context, out_full).astype(jnp.bfloat16), "tensor", scatter_dimension=0, tiled=True
    ).astype(jnp.float32)
    summed = inputs.astype(jnp.float32) + attention + out_bias
    normed = layer_norm(summed, norm1_gain, norm1_bias)
    normed_low = normed.astype(jnp.bfloat16)
    normed_all = lax.all_gather(normed_low, "tensor", axis=0, tiled=True)
    up_value = product(normed_all, up_rows) + up_bias
    active = gelu_tanh(up_value).astype(jnp.bfloat16)
    feed = lax.psum_scatter(
        product(active, down_cols).astype(jnp.bfloat16), "tensor", scatter_dimension=0, tiled=True
    ).astype(jnp.float32)
    pre_norm = normed + feed + down_bias
    layer_out = layer_norm(pre_norm, norm2_gain, norm2_bias).astype(jnp.bfloat16)
    _, norm2_pull = jax.vjp(layer_norm, pre_norm, norm2_gain, norm2_bias)
    grad_pre, grad_gain_two, grad_shift_two = norm2_pull(out_grad.astype(jnp.float32))
    grad_pre_low = grad_pre.astype(jnp.bfloat16)
    _, gelu_pull = jax.vjp(gelu_tanh, up_value)
    grad_pre_all = lax.all_gather(grad_pre_low, "tensor", axis=0, tiled=True)
    grad_up = gelu_pull(product_nt(grad_pre_all, down_cols))[0].astype(jnp.bfloat16)
    grad_down_local = product_tn(active, grad_pre_all)
    grad_up_local = product_tn(normed_all, grad_up)
    grad_normed_part = lax.psum_scatter(
        product_nt(grad_up, up_rows).astype(jnp.bfloat16), "tensor", scatter_dimension=0, tiled=True
    ).astype(jnp.float32)
    grad_up_bias_full = lax.dynamic_update_slice(
        jnp.zeros((local_hidden * tensor_size,), jnp.float32),
        jnp.sum(grad_up.astype(jnp.float32), axis=0),
        (tensor_rank * local_hidden,),
    )
    grad_normed = grad_pre + grad_normed_part
    _, norm1_pull = jax.vjp(layer_norm, summed, norm1_gain, norm1_bias)
    grad_summed, grad_gain_one, grad_shift_one = norm1_pull(grad_normed)
    grad_summed_low = grad_summed.astype(jnp.bfloat16)
    grad_summed_all = lax.all_gather(grad_summed_low, "tensor", axis=0, tiled=True)
    grad_out_local = product_tn(context, grad_summed_all)
    grad_context = product_nt(grad_summed_all, out_full).astype(jnp.bfloat16)
    grad_context_slots = to_slots(grad_context, slot_order)
    again_scores = masked_scores(query_slots, key_slots, segment_slots)
    prob_values = jnp.exp(again_scores - log_total)
    again_low = prob_values.astype(jnp.bfloat16)
    grad_prob = jnp.einsum(
        "hcqd,hckd->hcqk", grad_context_slots, value_slots, preferred_element_type=jnp.float32
    )
    grad_scores = (
        prob_values * (grad_prob - jnp.sum(prob_values * grad_prob, axis=-1, keepdims=True))
    ).astype(jnp.bfloat16)
    grad_query_slots = (
        jnp.einsum("hcqk,hckd->hcqd", grad_scores, key_slots, preferred_element_type=jnp.float32)
        * HD ** (-0.5)
    ).astype(jnp.bfloat16)
    grad_key_slots = (
        jnp.einsum("hcqk,hcqd->hckd", grad_scores, query_slots, preferred_element_type=jnp.float32)
        * HD ** (-0.5)
    ).astype(jnp.bfloat16)
    grad_value_slots = jnp.einsum(
        "hcqk,hcqd->hckd", again_low, grad_context_slots, preferred_element_type=jnp.float32
    ).astype(jnp.bfloat16)
    grad_query = to_tokens(grad_query_slots, token_place)
    grad_key = to_tokens(grad_key_slots, token_place)
    grad_value = to_tokens(grad_value_slots, token_place)
    grad_query_local = product_tn(inputs_all, grad_query)
    grad_key_local = product_tn(inputs_all, grad_key)
    grad_value_local = product_tn(inputs_all, grad_value)
    grad_inputs = grad_summed + lax.psum_scatter(
        (
            product_nt(grad_query, query_full)
            + product_nt(grad_key, key_full)
            + product_nt(grad_value, value_full)
        ).astype(jnp.bfloat16),
        "tensor",
        scatter_dimension=0,
        tiled=True,
    ).astype(jnp.float32)
    width_full = local_width * tensor_size

    def spread_width(part_sum):
        return lax.dynamic_update_slice(
            jnp.zeros((width_full,), jnp.float32), part_sum, (tensor_rank * local_width,)
        )

    (
        query_bias_sum,
        value_bias_sum,
        up_bias_sum,
        grad_out_bias,
        grad_norm1_gain,
        grad_norm1_bias,
        grad_down_bias,
        grad_norm2_gain,
        grad_norm2_bias,
    ) = lax.psum(
        (
            spread_width(jnp.sum(grad_query.astype(jnp.float32), axis=0)),
            spread_width(jnp.sum(grad_value.astype(jnp.float32), axis=0)),
            grad_up_bias_full,
            jnp.sum(grad_summed, axis=0),
            grad_gain_one,
            grad_shift_one,
            jnp.sum(grad_pre, axis=0),
            grad_gain_two,
            grad_shift_two,
        ),
        ("dp", "tensor"),
    )
    grad_query_bias = lax.dynamic_slice_in_dim(
        query_bias_sum, tensor_rank * local_width, local_width, 0
    )
    grad_value_bias = lax.dynamic_slice_in_dim(
        value_bias_sum, tensor_rank * local_width, local_width, 0
    )
    grad_up_bias = lax.dynamic_slice_in_dim(
        up_bias_sum, tensor_rank * local_hidden, local_hidden, 0
    )
    (
        grad_query_weight,
        grad_key_weight,
        grad_value_weight,
        grad_out_weight,
        grad_up_weight,
        grad_down_weight,
    ) = (
        lax.psum_scatter(grad_query_local, "dp", scatter_dimension=0, tiled=True),
        lax.psum_scatter(grad_key_local, "dp", scatter_dimension=0, tiled=True),
        lax.psum_scatter(grad_value_local, "dp", scatter_dimension=0, tiled=True),
        lax.psum_scatter(grad_out_local, "dp", scatter_dimension=1, tiled=True),
        lax.psum_scatter(grad_up_local, "dp", scatter_dimension=0, tiled=True),
        lax.psum_scatter(grad_down_local, "dp", scatter_dimension=1, tiled=True),
    )
    return (
        layer_out,
        grad_inputs,
        grad_query_weight,
        grad_query_bias,
        grad_key_weight,
        grad_value_weight,
        grad_value_bias,
        grad_out_weight,
        grad_out_bias,
        grad_norm1_gain,
        grad_norm1_bias,
        grad_up_weight,
        grad_up_bias,
        grad_down_weight,
        grad_down_bias,
        grad_norm2_gain,
        grad_norm2_bias,
    )


def solution(mesh):
    in_specs = (
        P(("dp", "tensor"), None),
        P(("dp", "tensor"), None),
        P("dp", None),
        P("dp", None),
        P("dp", "tensor", None),
        P("dp", "tensor"),
        P("tensor"),
        P("dp", "tensor"),
        P("dp", "tensor"),
        P("tensor"),
        P("tensor", "dp"),
        P(),
        P(),
        P(),
        P("dp", "tensor"),
        P("tensor"),
        P("tensor", "dp"),
        P(),
        P(),
        P(),
    )
    out_specs = (
        P(("dp", "tensor"), None),
        P(("dp", "tensor"), None),
        P("dp", "tensor"),
        P("tensor"),
        P("dp", "tensor"),
        P("dp", "tensor"),
        P("tensor"),
        P("tensor", "dp"),
        P(),
        P(),
        P(),
        P("dp", "tensor"),
        P("tensor"),
        P("tensor", "dp"),
        P(),
        P(),
        P(),
    )
    return jax.shard_map(local, mesh=mesh, in_specs=in_specs, out_specs=out_specs, check_vma=False)
```

profile of v0, /device:TPU:0, one launch (start us, length us, event | category | flops | bytes accessed | tf_op | source)
XLA Modules:
  0.0 1201.7 jit_solution(17774574574458499164)
XLA Ops:
  9.7 34.3 %gather_fusion = s32[6144]{0:T(1024)S(1)} fusion(s32[2048]{0:T(1024)S(1)} %bitcast.160, s32[6144]{0:T(1024)S(1)} %broadcast_clamp_fusion.1), kind=kCustom, calls=%fused_computation.clone | custom fusion | bytes 73728 | tf_op jit(solution)/shard_map/jit(_take)/gather | solution.py:98
  44.6 23.0 %scatter_custom_fusion = s32[6144]{0:T(1024)S(1)} fusion(s32[6144]{0:T(1024)S(1)} %reshape.282, s32[6144]{0:T(1024)S(1)} %reshape.284, s32[]{:T(128)} %constant.20.clone.1), kind=kCustom, calls=%fused_computation.120 | custom fusion | bytes 24580
  67.9 34.3 %gather_fusion.1 = s32[6144]{0:T(1024)S(1)} fusion(s32[2048]{0:T(1024)S(1)} %convert_reduce_fusion.4, s32[6144]{0:T(1024)S(1)} %broadcast_clamp_fusion), kind=kCustom, calls=%fused_computation.2.clone | custom fusion | bytes 73728 | tf_op jit(solution)/shard_map/jit(_take)/gather | solution.py:102
  102.4 12.1 %all_gather.34 = bf16[192,768]{0,1:T(8,128)(2,1)} all-gather(bf16[192,96]{0,1:T(8,128)(2,1)S(1)} %copy.132), channel_id=1, replica_groups=mesh['dp'=8,'tensor'=4] {'dp'}, dimensions={1}, use_global_device_ids=true | all-gather | bytes 331776 | tf_op jit(solution)/shard_map/all_gather | solution.py:91
  114.5 10.5 all_gather.31
  124.9 9.6 all_gather.32
  134.6 10.0 all_gather.33
  144.7 3.1 fusion.8
  148.7 32.3 %gather_fusion.4 = bf16[6144,64]{1,0:T(8,128)(2,1)S(1)} fusion(bf16[3,2048,64]{2,1,0:T(8,128)(2,1)S(1)} %bitcast.163, s32[6144]{0:T(1024)S(1)} %reshape.300), kind=kCustom, calls=%fused_computation.4.clone | custom fusion | bytes 1622016 | tf_op jit(solution)/shard_map/jit(take_along_axis)/gather | solution.py:40
  182.4 3.1 convolution_convert_fusion.4
  186.4 32.3 %gather_fusion.3 = bf16[6144,64]{1,0:T(8,128)(2,1)S(1)} fusion(bf16[3,2048,64]{2,1,0:T(8,128)(2,1)S(1)} %bitcast.164, s32[6144]{0:T(1024)S(1)} %reshape.300), kind=kCustom, calls=%fused_computation.3.clone | custom fusion | bytes 1622016 | tf_op jit(solution)/shard_map/jit(take_along_axis)/gather | solution.py:40
  220.1 3.1 fusion.7
  224.1 32.3 %gather_fusion.2 = bf16[6144,64]{1,0:T(8,128)(2,1)S(1)} fusion(bf16[3,2048,64]{2,1,0:T(8,128)(2,1)S(1)} %bitcast.165, s32[6144]{0:T(1024)S(1)} %reshape.300), kind=kCustom, calls=%fused_computation.1.clone | custom fusion | bytes 1622016 | tf_op jit(solution)/shard_map/jit(take_along_axis)/gather | solution.py:40
  257.0 1.6 select_bitcast_fusion.3
  258.7 3.2 fusion.46
  264.9 32.3 %gather_fusion.5 = bf16[6144,64]{1,0:T(8,128)(2,1)S(1)} fusion(bf16[3,2048,64]{2,1,0:T(8,128)(2,1)S(1)} %bitcast.166, s32[6144]{0:T(1024)S(1)} %reshape.312), kind=kCustom, calls=%fused_computation.5.clone | custom fusion | bytes 1622016 | tf_op jit(solution)/shard_map/jit(take_along_axis)/gather | solution.py:47
  299.0 2.7 convolution_convert_fusion.2
  302.5 59.9 %reduce-scatter.19.cloned.1.call-done = bf16[512,768]{1,0:T(8,128)(2,1)} async-done(((bf16[2048,768]{1,0:T(8,128)(2,1)}), bf16[512,768]{1,0:T(8,128)(2,1)}) %reduce-scatter.19.cloned.1.call-update) | async-done | bytes 786448 | tf_op jit(solution)/shard_map/reduce_scatter | solution.py:120
  362.4 1.5 fusion.15
  364.0 1.6 multiply_reduce_fusion.4
  367.6 62.8 %all-gather.9.cloned.1.call-done = bf16[2048,768]{1,0:T(8,128)(2,1)} async-done(((bf16[512,768]{1,0:T(8,128)(2,1)}), bf16[2048,768]{1,0:T(8,128)(2,1)}) %all-gather.9.cloned.1.call-update) | async-done | bytes 3145744 | tf_op jit(solution)/shard_map/all_gather | solution.py:126
  430.4 9.7 multiply_convert_fusion
  440.1 14.6 %all-gather.13.cloned.1.call-done = bf16[768,768]{0,1:T(8,128)(2,1)} async-done(((bf16[768,96]{0,1:T(8,128)(2,1)}), bf16[768,768]{0,1:T(8,128)(2,1)}) %all-gather.13.cloned.1.call-update) | async-done | bytes 1179664 | tf_op jit(solution)/shard_map/all_gather | solution.py:93
  454.7 6.5 convolution_convert_fusion.1
  461.4 60.3 %reduce-scatter.21.cloned.1.call-done = bf16[512,768]{1,0:T(8,128)(2,1)} async-done(((bf16[2048,768]{1,0:T(8,128)(2,1)}), bf16[512,768]{1,0:T(8,128)(2,1)}) %reduce-scatter.21.cloned.1.call-update) | async-done | bytes 786448 | tf_op jit(solution)/shard_map/reduce_scatter | solution.py:129
  521.7 1.9 fusion.45
  524.6 2.7 fusion.44
  528.6 63.3 %all-gather.15.cloned.1.call-done = bf16[2048,768]{1,0:T(8,128)(2,1)} async-done(((bf16[512,768]{1,0:T(8,128)(2,1)}), bf16[2048,768]{1,0:T(8,128)(2,1)}) %all-gather.15.cloned.1.call-update) | async-done | bytes 3145744 | tf_op jit(solution)/shard_map/all_gather | solution.py:138
  592.0 8.8 convert_reduce_fusion
  600.8 1.6 copy-done.52
  602.4 4.0 convolution_convert_fusion
  606.5 59.0 %reduce-scatter.23.cloned.1.call-done = bf16[512,768]{1,0:T(8,128)(2,1)} async-done(((bf16[2048,768]{1,0:T(8,128)(2,1)}), bf16[512,768]{1,0:T(8,128)(2,1)}) %reduce-scatter.23.cloned.1.call-update) | async-done | bytes 786448 | tf_op jit(solution)/shard_map/reduce_scatter | solution.py:142
  665.5 2.2 multiply_reduce_fusion.1
  671.4 63.3 %all-gather.17.cloned.1.call-done = bf16[2048,768]{1,0:T(8,128)(2,1)} async-done(((bf16[512,768]{1,0:T(8,128)(2,1)}), bf16[2048,768]{1,0:T(8,128)(2,1)}) %all-gather.17.cloned.1.call-update) | async-done | bytes 3145744 | tf_op jit(solution)/shard_map/all_gather | solution.py:154
  734.7 3.1 convolution_convert_fusion.3
  738.6 60.6 %gather_fusion.6 = bf16[6144,64]{1,0:T(8,128)(2,1)} fusion(bf16[3,2048,64]{2,1,0:T(8,128)(2,1)S(1)} %bitcast.161, s32[6144]{0:T(1024)S(1)} %reshape.300), kind=kCustom, calls=%fused_computation.6.clone | custom fusion | bytes 1622016 | tf_op jit(solution)/shard_map/jit(take_along_axis)/gather | solution.py:40
  799.2 2.6 copy.134
  801.7 4.3 convolution_convert_fusion.6
  808.2 2.1 multiply_convert_fusion.2
  810.3 1.5 multiply_convert_fusion.3
  811.8 2.2 convolution_bitcast_fusion
  815.4 32.3 %gather_fusion.9 = bf16[6144,64]{1,0:T(8,128)(2,1)S(1)} fusion(bf16[3,2048,64]{2,1,0:T(8,128)(2,1)S(1)} %bitcast.167, s32[6144]{0:T(1024)S(1)} %reshape.312), kind=kCustom, calls=%fused_computation.9.clone | custom fusion | bytes 1622016 | tf_op jit(solution)/shard_map/jit(take_along_axis)/gather | solution.py:47
  849.1 1.8 copy.160
  850.9 32.3 %gather_fusion.7 = bf16[6144,64]{1,0:T(8,128)(2,1)S(1)} fusion(bf16[3,2048,64]{2,1,0:T(8,128)(2,1)S(1)} %bitcast.168, s32[6144]{0:T(1024)S(1)} %reshape.312), kind=kCustom, calls=%fused_computation.7.clone | custom fusion | bytes 1622016 | tf_op jit(solution)/shard_map/jit(take_along_axis)/gather | solution.py:47
  884.7 1.8 copy.161
  886.5 32.3 %gather_fusion.8 = bf16[6144,64]{1,0:T(8,128)(2,1)S(1)} fusion(bf16[3,2048,64]{2,1,0:T(8,128)(2,1)S(1)} %bitcast.162, s32[6144]{0:T(1024)S(1)} %reshape.312), kind=kCustom, calls=%fused_computation.8.clone | custom fusion | bytes 1622016 | tf_op jit(solution)/shard_map/jit(take_along_axis)/gather | solution.py:47
  923.3 2.8 add_convert_fusion
  926.1 1.8 copy-done.46
  928.0 6.0 fusion.49
  934.3 7.1 fusion.50
  941.4 2.8 convolution_bitcast_fusion.1
  944.2 2.2 copy.167
  946.5 2.8 convolution_bitcast_fusion.3
  949.3 2.2 copy.163
  951.6 2.8 convolution_bitcast_fusion.2
  954.4 2.3 copy.165
  957.6 43.1 %all-reduce = (f32[768]{0:T(1024)S(1)}, f32[768]{0:T(1024)S(1)}, f32[768]{0:T(1024)}, f32[768]{0:T(1024)}, f32[768]{0:T(1024)}, /*index=5*/f32[3072]{0:T(1024)S(1)}, f32[768]{0:T(1024)}, f32[768]{0:T(1024)}, f32[768]{0:T(1024)}) all-reduce(f32[768]{0:T(1024)S(1)} %dynamic_update_slice.9, ...), channel_id=1, replica_groups=mesh['dp'=8,'tensor'=4] {'dp','tensor'}, use_global_device_ids=true, to_apply=%region_20.23 | all-reduce | flops 9216 | bytes 73728 | tf_op jit(solution)/shard_map/psum | solution.py:211
  1002.6 1.6 copy.170
  1004.3 2.5 convert_add_fusion
  1006.8 25.1 %reduce-scatter.27.cloned.1.call-done = f32[96,768]{1,0:T(8,128)} async-done(((f32[768,768]{1,0:T(8,128)}), f32[96,768]{1,0:T(8,128)}) %reduce-scatter.27.cloned.1.call-update) | async-done | bytes 294928 | tf_op jit(solution)/shard_map/reduce_scatter | solution.py:246
  1031.9 46.5 %reduce-scatter.29.cloned.1.call-done = f32[768,96]{0,1:T(8,128)} async-done(((f32[768,768]{0,1:T(8,128)}), f32[768,96]{0,1:T(8,128)}) %reduce-scatter.29.cloned.1.call-update) | async-done | bytes 294928 | tf_op jit(solution)/shard_map/reduce_scatter | solution.py:247
  1078.4 38.7 %reduce-scatter.35.cloned.1.call-done = f32[96,192]{1,0:T(8,128)} async-done(((f32[768,192]{1,0:T(8,128)}), f32[96,192]{1,0:T(8,128)}) %reduce-scatter.35.cloned.1.call-update) | async-done | bytes 73744
  1117.1 38.6 %reduce-scatter.31.cloned.1.call-done = f32[96,192]{1,0:T(8,128)} async-done(((f32[768,192]{1,0:T(8,128)}), f32[96,192]{1,0:T(8,128)}) %reduce-scatter.31.cloned.1.call-update) | async-done | bytes 73744
  1155.7 38.7 %reduce-scatter.33.cloned.1.call-done = f32[96,192]{1,0:T(8,128)} async-done(((f32[768,192]{1,0:T(8,128)}), f32[96,192]{1,0:T(8,128)}) %reduce-scatter.33.cloned.1.call-update) | async-done | bytes 73744
  (216 shorter events, 37.2 us)
Async XLA Ops:
  8.0 1.6 copy-start
  8.0 136.6 %all-gather.7.cloned.1.call-start = ((), (), s32[]{:S(2)}) async-start(), calls=%async_computation.10 | async-start | bytes 3932160 | tf_op jit(solution)/shard_map/all_gather | solution.py:105
  8.8 353.6 %reduce-scatter.19.cloned.1.call-start = ((), (), s32[]{:S(2)}) async-start(), calls=%async_computation.11 | async-start | bytes 3932160 | tf_op jit(solution)/shard_map/reduce_scatter | solution.py:120
  9.6 34.4 %copy-start.34 = (s32[1,3,2048]{2,0,1:T(1,128)S(1)}, s32[1,3,2048]{2,0,1:T(1,128)}, u32[]{:S(2)}) copy-start(s32[1,3,2048]{2,0,1:T(1,128)} %param.28) | copy-start | bytes 73732
  9.6 34.5 %copy-start.44 = (s32[2]{0:T(128)S(1)}, s32[2]{0:T(128)}, u32[]{:S(2)}) copy-start(s32[2]{0:T(128)} %constant.77) | copy-start | bytes 28
  9.7 34.5 %copy-start.45 = (s32[2]{0:T(128)S(1)}, s32[2]{0:T(128)}, u32[]{:S(2)}) copy-start(s32[2]{0:T(128)} %constant.80) | copy-start | bytes 28
  9.7 34.7 %copy-start.51 = (s32[1,3]{1,0:T(1,128)S(1)}, s32[1,3]{1,0:T(1,128)}, u32[]{:S(2)}) copy-start(s32[1,3]{1,0:T(1,128)} %param.26) | copy-start | bytes 40
  67.9 34.4 %copy-start.39 = (bf16[192,96]{1,0:T(8,128)(2,1)S(1)}, bf16[192,96]{1,0:T(8,128)(2,1)}, u32[]{:S(2)}) copy-start(bf16[192,96]{1,0:T(8,128)(2,1)} %param.34) | copy-start | bytes 110596
  67.9 46.6 %copy-start.36 = (bf16[96,192]{1,0:T(8,128)(2,1)S(1)}, bf16[96,192]{1,0:T(8,128)(2,1)}, u32[]{:S(2)}) copy-start(bf16[96,192]{1,0:T(8,128)(2,1)} %param.29) | copy-start | bytes 110596
  67.9 57.0 %copy-start.37 = (bf16[96,192]{1,0:T(8,128)(2,1)S(1)}, bf16[96,192]{1,0:T(8,128)(2,1)}, u32[]{:S(2)}) copy-start(bf16[96,192]{1,0:T(8,128)(2,1)} %param.31) | copy-start | bytes 110596
  67.9 66.7 %copy-start.38 = (bf16[96,192]{1,0:T(8,128)(2,1)S(1)}, bf16[96,192]{1,0:T(8,128)(2,1)}, u32[]{:S(2)}) copy-start(bf16[96,192]{1,0:T(8,128)(2,1)} %param.32) | copy-start | bytes 110596
  67.9 76.8 %copy-start.49 = (f32[192]{0:T(256)S(1)}, f32[192]{0:T(256)}, u32[]{:S(2)}) copy-start(f32[192]{0:T(256)} %param.33) | copy-start | bytes 2308
  144.6 3.2 copy-start.31
  186.4 33.7 %copy-start.50 = (f32[192]{0:T(256)S(1)}, f32[192]{0:T(256)}, u32[]{:S(2)}) copy-start(f32[192]{0:T(256)} %param.30) | copy-start | bytes 2308
  258.6 3.9 copy-start.19
  258.7 3.9 copy-start.21
  258.7 3.9 copy-start.12
  261.8 1.7 copy-start.2
  297.2 1.7 copy-start.16
  299.0 63.5 %copy-start.5 = (bf16[512,768]{1,0:T(8,128)(2,1)S(1)}, bf16[512,768]{1,0:T(8,128)(2,1)}, u32[]{:S(2)}) copy-start(bf16[512,768]{1,0:T(8,128)(2,1)} %param.24) | copy-start | bytes 2359300
  299.0 63.5 %copy-start.33 = (f32[768]{0:T(1024)S(1)}, f32[768]{0:T(1024)}, u32[]{:S(2)}) copy-start(f32[768]{0:T(1024)} %param.35) | copy-start | bytes 9220
  301.7 63.9 %copy-start.35 = (f32[768]{0:T(1024)S(1)}, f32[768]{0:T(1024)}, u32[]{:S(2)}) copy-start(f32[768]{0:T(1024)} %param.36) | copy-start | bytes 9220
  301.7 63.9 %copy-start.41 = (f32[768]{0:T(1024)S(1)}, f32[768]{0:T(1024)}, u32[]{:S(2)}) copy-start(f32[768]{0:T(1024)} %param.37) | copy-start | bytes 9220
  301.7 65.9 %all-gather.11.cloned.1.call-start = ((), (), s32[]{:S(2)}) async-start(), calls=%async_computation.13 | async-start | bytes 1327104 | tf_op jit(solution)/shard_map/all_gather | solution.py:92
  302.3 128.1 %copy-start.48 = (f32[768]{0:T(1024)S(1)}, f32[768]{0:T(1024)}, u32[]{:S(2)}) copy-start(f32[768]{0:T(1024)} %param.39) | copy-start | bytes 9220
  302.3 128.1 %all-gather.9.cloned.1.call-start = ((), (), s32[]{:S(2)}) async-start(), calls=%async_computation.12 | async-start | bytes 3932160 | tf_op jit(solution)/shard_map/all_gather | solution.py:126
  362.4 3.2 copy-start.6
  366.9 87.8 %all-gather.13.cloned.1.call-start = ((), (), s32[]{:S(2)}) async-start(), calls=%async_computation.14 | async-start | bytes 1327104 | tf_op jit(solution)/shard_map/all_gather | solution.py:93
  367.5 154.1 %reduce-scatter.21.cloned.1.call-start = ((), (), s32[]{:S(2)}) async-start(), calls=%async_computation.15 | async-start | bytes 3932160 | tf_op jit(solution)/shard_map/reduce_scatter | solution.py:129
  461.3 60.4 %copy-start.43 = (f32[768]{0:T(1024)S(1)}, f32[768]{0:T(1024)}, u32[]{:S(2)}) copy-start(f32[768]{0:T(1024)} %param.41) | copy-start | bytes 9220
  461.3 62.6 %copy-start.18 = (bf16[512,768]{1,0:T(8,128)(2,1)S(1)}, bf16[512,768]{1,0:T(8,128)(2,1)}, u32[]{:S(2)}) copy-start(bf16[512,768]{1,0:T(8,128)(2,1)} %param.25) | copy-start | bytes 2359300
  461.3 62.6 %copy-start.40 = (f32[768]{0:T(1024)S(1)}, f32[768]{0:T(1024)}, u32[]{:S(2)}) copy-start(f32[768]{0:T(1024)} %param.42) | copy-start | bytes 9220
  461.3 63.3 %copy-start.42 = (f32[768]{0:T(1024)S(1)}, f32[768]{0:T(1024)}, u32[]{:S(2)}) copy-start(f32[768]{0:T(1024)} %param.43) | copy-start | bytes 9220
  461.3 130.6 %all-gather.15.cloned.1.call-start = ((), (), s32[]{:S(2)}) async-start(), calls=%async_computation.16 | async-start | bytes 3932160 | tf_op jit(solution)/shard_map/all_gather | solution.py:138
  528.4 137.1 %reduce-scatter.23.cloned.1.call-start = ((), (), s32[]{:S(2)}) async-start(), calls=%async_computation.17 | async-start | bytes 3932160 | tf_op jit(solution)/shard_map/reduce_scatter | solution.py:142
  592.0 10.4 copy-start.47
  600.8 1.6 copy-start.52
  606.5 128.2 %all-gather.17.cloned.1.call-start = ((), (), s32[]{:S(2)}) async-start(), calls=%async_computation.18 | async-start | bytes 3932160 | tf_op jit(solution)/shard_map/all_gather | solution.py:154
  665.5 2.3 copy-start.24
  668.8 1.2 copy-start.7
  668.8 65.9 %copy-start.17 = (bf16[192,768]{0,1:T(8,128)(2,1)S(1)}, bf16[192,768]{0,1:T(8,128)(2,1)}, u32[]{:S(2)}) copy-start(bf16[192,768]{0,1:T(8,128)(2,1)} %all_gather.34) | copy-start | bytes 884740
  671.1 331.5 %reduce-scatter.37.cloned.1.call-start = ((), (), s32[]{:S(2)}) async-start(), calls=%async_computation.25 | async-start | bytes 884736
  799.2 6.9 copy-start.3
  801.7 4.3 copy-start.13
  801.7 4.3 copy-start.14
  808.2 2.1 copy-start.20
  808.2 3.6 copy-start.25
  808.2 3.6 copy-start.29
  811.8 2.8 copy-start.23
  814.0 190.2 %reduce-scatter.25.cloned.1.call-start = ((), (), s32[]{:S(2)}) async-start(), calls=%async_computation.19 | async-start | bytes 3932160 | tf_op jit(solution)/shard_map/reduce_scatter | solution.py:184
  919.6 1.3 copy-start.9
  919.8 1.2 copy-start.26
  919.8 1.4 copy-start.27
  921.8 1.5 copy-start.10
  921.8 1.5 copy-start.11
  926.1 1.9 copy-start.46
  926.1 105.8 %reduce-scatter.27.cloned.1.call-start = ((), (), s32[]{:S(2)}) async-start(), calls=%async_computation.20 | async-start | bytes 2654208 | tf_op jit(solution)/shard_map/reduce_scatter | solution.py:246
  934.0 7.4 copy-start.4
  934.0 144.4 %reduce-scatter.29.cloned.1.call-start = ((), (), s32[]{:S(2)}) async-start(), calls=%async_computation.21 | async-start | bytes 2654208 | tf_op jit(solution)/shard_map/reduce_scatter | solution.py:247
  941.3 175.8 %reduce-scatter.35.cloned.1.call-start = ((), (), s32[]{:S(2)}) async-start(), calls=%async_computation.24 | async-start | bytes 884736
  946.4 209.3 %reduce-scatter.31.cloned.1.call-start = ((), (), s32[]{:S(2)}) async-start(), calls=%async_computation.22 | async-start | bytes 884736
  951.5 242.9 %reduce-scatter.33.cloned.1.call-start = ((), (), s32[]{:S(2)}) async-start(), calls=%async_computation.23 | async-start | bytes 884736
  951.6 242.9 %copy-start.1 = (s32[1,2048]{1,0:T(1,128)S(1)}, s32[1,2048]{1,0:T(1,128)}, u32[]{:S(2)}) copy-start(s32[1,2048]{1,0:T(1,128)} %param.27) | copy-start | bytes 24580
  954.4 49.9 %copy-start.8 = (f32[512,768]{1,0:T(8,128)S(1)}, f32[512,768]{1,0:T(8,128)}, u32[]{:S(2)}) copy-start(f32[512,768]{1,0:T(8,128)} %copy-done.7) | copy-start | bytes 4718596
  (5 other events, 5.2 us)
Sparse Core Ops, SparseCore 0:
  10.4 66.1 all-gather.6
  301.8 60.5 reduce-scatter.18
  528.5 63.4 all-gather.14
  671.2 63.4 all-gather.16
Sparse Core Ops, SparseCore 1:
  304.1 24.1 all-gather.10
  367.0 63.3 all-gather.8
  432.2 22.5 all-gather.12
  461.4 60.2 reduce-scatter.20
  606.6 58.9 reduce-scatter.22
  814.1 33.5 reduce-scatter.36
  926.2 59.5 reduce-scatter.24
  989.6 42.3 reduce-scatter.26
  1036.1 42.3 reduce-scatter.28
  1082.2 34.9 reduce-scatter.34
  1120.7 34.9 reduce-scatter.30
  1159.4 34.9 reduce-scatter.32
where the time goes:
time: 1210 us; the launch traced here: 1200 us
  waiting for transfers between devices  573 us (47%)
  local copies, waits for them, and re-layouts  417 us (34%)
  matrix products  85.4 us (7%)
  blocking collectives  85.3 us (7%)
  other arithmetic  23.4 us (2%)
  between operations  16.5 us (1%)
    gather x9, local copies, waits for them, and re-layouts, to_slots(): picked = jnp.take_along_axis(per_head, slot_order[:, :, None], axis=1)  164 us
    gather x9, local copies, waits for them, and re-layouts, to_tokens(): placed = jnp.take_along_axis(flat_slots, token_place[:, :, None], axis=1)  133 us
    unnamed x20, waiting for transfers between devices  118 us
    all_gather x1, waiting for transfers between devices, local(): grad_pre_all = lax.all_gather(grad_pre_low, 'tensor', axis=0, tiled=True)  63.3 us
    all_gather x1, waiting for transfers between devices, local(): lax.all_gather(grad_summed_low, 'tensor', axis=0, tiled=True)  63.3 us
    all_gather x1, waiting for transfers between devices, local(): normed_all = lax.all_gather(normed_low, 'tensor', axis=0, tiled=True)  62.8 us
    reduce_scatter x1, waiting for transfers between devices, local(): lax.psum_scatter(product(active, down_cols).astype(jnp.bfloat16), 'tensor...  60.3 us
    reduce_scatter x1, waiting for transfers between devices, local(): lax.psum_scatter(product(context, out_full).astype(jnp.bfloat16), 'tensor...  59.9 us
  transfers between devices with their start and end apart: 16, of which 12 were waited for; matrix products, arithmetic and copies ran while one was open for 21% of the time, Pallas kernels for 0%

commit v1 on v0

v1 whole, which is shorter than its diff:
```python
import functools

import jax
import jax.numpy as jnp
from jax import lax
from jax.experimental import pallas as pl
from jax.experimental.pallas import tpu as pltpu
from jax.sharding import Mesh, PartitionSpec as P

HD = 64
CL = 128
BLK = 256
F32 = jnp.float32
BF16 = jnp.bfloat16
EPS = 1e-06


def nn(left, right):
    return jnp.dot(left, right, preferred_element_type=F32)


def nt(left, right):
    return lax.dot_general(left, right, (((1,), (1,)), ((), ())), preferred_element_type=F32)


def tn(left, right):
    return lax.dot_general(left, right, (((0,), (0,)), ((), ())), preferred_element_type=F32)


def order_kernel(seqs, scal_ref, clusters_ref, balance_ref, order_ref, seg_ref):
    count = balance_ref.shape[1]
    rows = scal_ref[1]
    balance = balance_ref[...]
    high = balance // 64
    low = balance - high * 64
    pick = lax.broadcasted_iota(jnp.int32, (8, count), 0)
    table = jnp.where(pick == 0, high, jnp.where(pick == 1, low, 0)).astype(F32).astype(BF16)
    chosen = clusters_ref[0]
    total = jnp.zeros((8, count), F32)
    for start in range(0, count, BLK):
        place = lax.broadcasted_iota(jnp.int32, (BLK, count), 0) + start
        hot = jnp.where(place == chosen, 1.0, 0.0).astype(BF16)
        total = total + nn(table[:, start : start + BLK], hot)
    token = (total[0:1] * 64.0 + total[1:2]).astype(jnp.int32)
    segment = jnp.zeros_like(token)
    for s in range(seqs):
        segment = segment + jnp.where(token >= scal_ref[2 + s], 1, 0)
    seg_ref[0] = segment.astype(F32)
    shift = scal_ref[0] * rows
    from_own = shift - (token // rows) * rows
    from_own = jnp.where(from_own < 0, from_own + count, from_own)
    order_ref[0] = (from_own + token % rows).astype(F32)


def column(row):
    return jnp.transpose(jnp.broadcast_to(row, (CL, CL)))


def slots_by_tokens(order_ref, start, count):
    lane = lax.broadcasted_iota(jnp.int32, (CL, CL), 1).astype(F32)
    parts = []
    for half in range(BLK // CL):
        gap = column(order_ref[0, :, pl.ds(start + half * CL, CL)]) - lane
        parts.append(
            jnp.concatenate(
                [jnp.where(gap == float(j * CL), 1.0, 0.0).astype(BF16) for j in range(count // CL)],
                axis=1,
            )
        )
    return jnp.concatenate(parts, axis=0)


def tokens_by_slots(order_ref, start, count):
    row = order_ref[0] - jnp.asarray(start, F32)
    place = lax.broadcasted_iota(jnp.int32, (BLK, count), 0).astype(F32)
    return jnp.where(place == row, 1.0, 0.0).astype(BF16)


def softmax_of(first, second, seg_ref, start):
    scores = nt(first, second) * HD ** (-0.5)
    seg_row = seg_ref[0, :, pl.ds(start, CL)]
    scores = jnp.where(column(seg_row) == seg_row, scores, -1e30)
    raised = jnp.exp(scores - jnp.max(scores, axis=1, keepdims=True))
    return raised / jnp.sum(raised, axis=1, keepdims=True)


def upper_half(values):
    lane = lax.broadcasted_iota(jnp.int32, values.shape, 1)
    return jnp.where(lane >= HD, values, 0.0)


def forward_kernel(blocks, order_ref, seg_ref, x_ref, w_ref, b_ref, slots_ref, out_ref, qkv_ref, ctx_ref):
    count = x_ref.shape[0]
    for start in range(0, count, BLK):
        qkv_ref[start : start + BLK] = (nn(x_ref[start : start + BLK], w_ref[0]) + b_ref[0]).astype(BF16)

    def gather(i, carry):
        start = pl.multiple_of(i * BLK, BLK)
        hot = slots_by_tokens(order_ref, start, count)
        picked = nn(hot, qkv_ref[...]).astype(BF16)
        slots_ref[0, pl.ds(start, BLK)] = picked
        for half in range(BLK // CL):
            part = picked[half * CL : (half + 1) * CL]
            first, second = part[:, :CL], part[:, CL:]
            probs = softmax_of(first, second, seg_ref, start + half * CL)
            context = nn(probs.astype(BF16), first)
            ctx_ref[pl.ds(start + half * CL, CL)] = upper_half(context).astype(BF16)
        return carry

    lax.fori_loop(0, count // BLK, gather, 0)
    rows = count // blocks

    def give(i, carry):
        def one(start):
            return nn(tokens_by_slots(order_ref, start, count), ctx_ref[...])

        for r in range(0, rows // 2, BLK):
            base = i * rows + r
            packed = pltpu.roll(one(base), HD, 1) + one(base + rows // 2)
            out_ref[i, r : r + BLK] = packed.astype(BF16)
        return carry

    lax.fori_loop(0, blocks, give, 0)


def backward_kernel(blocks, order_ref, seg_ref, slots_ref, g_ref, out_ref, gctx_ref, grad_ref):
    count = slots_ref.shape[1]
    rows = count // blocks
    half_rows = rows // 2
    for k in range(blocks):
        packed = g_ref[k].astype(F32)
        gctx_ref[k * rows : k * rows + half_rows] = upper_half(pltpu.roll(packed, HD, 1)).astype(BF16)
        gctx_ref[k * rows + half_rows : (k + 1) * rows] = upper_half(packed).astype(BF16)

    def gather(i, carry):
        start = pl.multiple_of(i * BLK, BLK)
        hot = slots_by_tokens(order_ref, start, count)
        picked = nn(hot, gctx_ref[...]).astype(BF16)
        for half in range(BLK // CL):
            at = start + half * CL
            part = slots_ref[0, pl.ds(at, CL)]
            first, second = part[:, :CL], part[:, CL:]
            grad_ctx = picked[half * CL : (half + 1) * CL]
            probs = softmax_of(first, second, seg_ref, at)
            grad_prob = nt(grad_ctx, first)
            inner = jnp.sum(probs * grad_prob, axis=1, keepdims=True)
            grad_scores = (probs * (grad_prob - inner)).astype(BF16)
            grad_query = nn(grad_scores, second) * HD ** (-0.5)
            grad_key = tn(grad_scores, first) * HD ** (-0.5)
            grad_value = tn(probs.astype(BF16), grad_ctx)
            lane = lax.broadcasted_iota(jnp.int32, (CL, CL), 1)
            grad_ref[pl.ds(at, CL), :CL] = jnp.where(lane < HD, grad_query, grad_value).astype(BF16)
            grad_ref[pl.ds(at, CL), CL:] = jnp.where(lane < HD, grad_key, 0.0).astype(BF16)
        return carry

    lax.fori_loop(0, count // BLK, gather, 0)

    def give(i, carry):
        def one(start):
            return nn(tokens_by_slots(order_ref, start, count), grad_ref[...])

        for r in range(0, half_rows, BLK):
            base = i * rows + r
            low, high = one(base), one(base + half_rows)
            out_ref[i, r : r + BLK] = low[:, :CL].astype(BF16)
            out_ref[i, half_rows + r : half_rows + r + BLK] = high[:, :CL].astype(BF16)
            packed = low[:, CL:] + pltpu.roll(high[:, CL:], HD, 1)
            out_ref[i, rows + r : rows + r + BLK] = packed.astype(BF16)
        return carry

    lax.fori_loop(0, blocks, give, 0)


def head_spec(shape, head):
    return pl.BlockSpec((1,) + shape, lambda i: (head,) + (0,) * len(shape))


def full_spec(shape):
    return pl.BlockSpec(shape, lambda i: (0,) * len(shape))


def params():
    return pltpu.CompilerParams(vmem_limit_bytes=48 * 1024 * 1024)


def slot_tokens(seqs, scalars, clusters, balance):
    heads, count = clusters.shape[0], clusters.shape[2]
    return pl.pallas_call(
        functools.partial(order_kernel, seqs),
        grid=(heads,),
        in_specs=[
            pl.BlockSpec(memory_space=pltpu.SMEM),
            pl.BlockSpec((1, 1, count), lambda h: (h, 0, 0)),
            pl.BlockSpec((1, count), lambda h: (0, 0)),
        ],
        out_specs=[pl.BlockSpec((1, 1, count), lambda h: (h, 0, 0))] * 2,
        out_shape=[jax.ShapeDtypeStruct((heads, 1, count), F32)] * 2,
        compiler_params=params(),
        name="slot_tokens",
        cost_estimate=pl.CostEstimate(flops=2 * 8 * heads * count * count, bytes_accessed=heads * count * 16, transcendentals=0),
    )(scalars, clusters, balance)


def attend(blocks, head, order, seg, x_all, weights, biases):
    count = x_all.shape[0]
    width = x_all.shape[1]
    rows = count // blocks
    return pl.pallas_call(
        functools.partial(forward_kernel, blocks),
        grid=(1,),
        in_specs=[
            head_spec((1, count), head),
            head_spec((1, count), head),
            full_spec((count, width)),
            head_spec((width, 2 * CL), head),
            head_spec((1, 2 * CL), head),
        ],
        out_specs=[full_spec((1, count, 2 * CL)), full_spec((blocks, rows // 2, CL))],
        out_shape=[
            jax.ShapeDtypeStruct((1, count, 2 * CL), BF16),
            jax.ShapeDtypeStruct((blocks, rows // 2, CL), BF16),
        ],
        scratch_shapes=[pltpu.VMEM((count, 2 * CL), BF16), pltpu.VMEM((count, CL), BF16)],
        compiler_params=params(),
        name="attend",
        cost_estimate=pl.CostEstimate(
            flops=2 * count * count * 3 * CL + 2 * count * width * 2 * CL, bytes_accessed=count * width * 2 + count * CL * 6, transcendentals=count * CL
        ),
    )(order, seg, x_all, weights, biases)


def attend_back(blocks, head, order, seg, slots, grad_context):
    count = slots.shape[1]
    rows = count // blocks
    return pl.pallas_call(
        functools.partial(backward_kernel, blocks),
        grid=(1,),
        in_specs=[
            head_spec((1, count), head),
            head_spec((1, count), head),
            full_spec((1, count, 2 * CL)),
            full_spec((blocks, rows // 2, CL)),
        ],
        out_specs=full_spec((blocks, rows + rows // 2, CL)),
        out_shape=jax.ShapeDtypeStruct((blocks, rows + rows // 2, CL), BF16),
        scratch_shapes=[pltpu.VMEM((count, CL), BF16), pltpu.VMEM((count, 2 * CL), BF16)],
        compiler_params=params(),
        name="attend_back",
        cost_estimate=pl.CostEstimate(flops=2 * count * count * 3 * CL, bytes_accessed=count * CL * 12, transcendentals=count * CL),
    )(order, seg, slots, grad_context)


def norm_stats(values_in):
    center = values_in - jnp.mean(values_in, axis=-1, keepdims=True)
    inverse = lax.rsqrt(jnp.mean(center * center, axis=-1, keepdims=True) + EPS)
    return center * inverse, inverse


def norm_back(cotangent, gain, hat, inverse):
    scaled = cotangent * gain
    return inverse * (
        scaled
        - jnp.mean(scaled, axis=-1, keepdims=True)
        - hat * jnp.mean(scaled * hat, axis=-1, keepdims=True)
    )


def exchange(parts, size, sign):
    return [parts[0]] + [
        lax.ppermute(parts[k], "tensor", [(i, (i + sign * k) % size) for i in range(size)])
        for k in range(1, size)
    ]


def gather_line(own, size, rank):
    up, down = own, own
    ups, downs = [], []
    for k in range(1, size):
        up = lax.ppermute(up, "tensor", [(i, i + 1) for i in range(k - 1, size - 1)])
        down = lax.ppermute(down, "tensor", [(i + 1, i) for i in range(0, size - k)])
        ups.append(up)
        downs.append(down)
    return [own] + [jnp.where(rank >= k, ups[k - 1], downs[size - 1 - k]) for k in range(1, size)]


def local(
    inputs, out_grad, seq_lengths, balance, clusters, query_weight, query_bias, key_weight,
    value_weight, value_bias, out_weight, out_bias, norm1_gain, norm1_bias, up_weight, up_bias,
    down_weight, down_bias, norm2_gain, norm2_bias,
):
    dp = ("chip", "core")
    everyone = ("chip", "core", "tensor")
    rows, width = inputs.shape
    size = lax.axis_size("tensor")
    rank = lax.axis_index("tensor")
    dp_size = lax.axis_size("chip") * lax.axis_size("core")
    shard = query_weight.shape[0]
    local_width = query_weight.shape[1]
    local_hidden = up_weight.shape[1]
    heads = clusters.shape[1]
    seqs = seq_lengths.shape[1]

    bounds = jnp.cumsum(seq_lengths[0])
    scalars = jnp.concatenate([jnp.stack([rank, jnp.int32(rows)]), bounds]).astype(jnp.int32)
    order, seg = slot_tokens(seqs, scalars, clusters[0][:, None, :], balance)

    own_qkv = lax.all_gather(
        jnp.concatenate([query_weight, key_weight, value_weight], axis=1), dp, axis=0, tiled=True
    )
    pieces = own_qkv.reshape(width, 3, heads, HD)
    head_weights = jnp.concatenate(
        [pieces[:, 0], pieces[:, 2], pieces[:, 1], jnp.zeros_like(pieces[:, 0])], axis=-1
    ).transpose(1, 0, 2)
    no_bias = jnp.zeros((heads, HD), F32)
    head_biases = jnp.concatenate(
        [query_bias.reshape(heads, HD), value_bias.reshape(heads, HD), no_bias, no_bias], axis=-1
    )[:, None, :]
    ff = lax.all_gather(
        jnp.concatenate([up_weight, down_weight.T, out_weight.T], axis=1), everyone, axis=0, tiled=True
    ).reshape(dp_size, size, shard, 2 * local_hidden + local_width)

    def whole(start, stop):
        return ff[:, :, :, start:stop].transpose(0, 2, 1, 3).reshape(width, size * (stop - start))

    up_full = whole(0, local_hidden)
    down_full_t = whole(local_hidden, 2 * local_hidden)
    out_full_t = whole(2 * local_hidden, 2 * local_hidden + local_width)
    up_bias_full = lax.all_gather(up_bias, "tensor", axis=0, tiled=True)

    x_parts = gather_line(inputs, size, rank)
    x_all = jnp.concatenate(x_parts, axis=0)

    slots, contexts = [], []
    for h in range(heads):
        kept, context_h = attend(size, h, order, seg, x_all, head_weights, head_biases)
        slots.append(kept)
        contexts.append(exchange([context_h[k] for k in range(size)], size, -1))
    packed = jnp.stack([jnp.stack([contexts[h][k] for h in range(heads)]) for k in range(size)])
    context = (
        packed.reshape(size, heads, rows // 2, 2, HD)
        .transpose(3, 2, 0, 1, 4)
        .reshape(rows, size, heads * HD)
    )
    doubled = jnp.concatenate([context, context], axis=1)
    context = lax.dynamic_slice_in_dim(doubled, (size - rank) % size, size, 1).reshape(rows, width)

    summed = inputs.astype(F32) + nt(context, out_full_t) + out_bias
    hat1, inverse1 = norm_stats(summed)
    normed = hat1 * norm1_gain + norm1_bias
    normed_low = normed.astype(BF16)
    up_value = nn(normed_low, up_full) + up_bias_full
    curve = 2.0**0.5 * (1.0 / jnp.pi) ** 0.5
    square = up_value * up_value
    tanh = jnp.tanh(curve * (up_value + 0.044715 * square * up_value))
    active = (0.5 * up_value * (1.0 + tanh)).astype(BF16)
    slope = 0.5 * (1.0 + tanh) + 0.5 * up_value * (1.0 - tanh * tanh) * curve * (1.0 + 3 * 0.044715 * square)
    pre_norm = normed + nt(active, down_full_t) + down_bias
    hat2, inverse2 = norm_stats(pre_norm)
    layer_out = (hat2 * norm2_gain + norm2_bias).astype(BF16)
    cot = out_grad.astype(F32)
    grad_pre = norm_back(cot, norm2_gain, hat2, inverse2)
    grad_pre_low = grad_pre.astype(BF16)
    grad_down_t = tn(grad_pre_low, active).astype(BF16)
    grad_up = (nn(grad_pre_low, down_full_t) * slope).astype(BF16)
    grad_up_w = tn(normed_low, grad_up).astype(BF16)
    grad_normed = grad_pre + nt(grad_up, up_full)
    grad_summed = norm_back(grad_normed, norm1_gain, hat1, inverse1)
    grad_summed_low = grad_summed.astype(BF16)
    grad_out_t = tn(grad_summed_low, context).astype(BF16)
    grad_context = nn(grad_summed_low, out_full_t).astype(BF16)

    grad_context = grad_context.reshape(rows, size, heads * HD)
    grad_context = lax.dynamic_slice_in_dim(
        jnp.concatenate([grad_context, grad_context], axis=1), rank, size, 1
    )
    grad_packed = (
        grad_context.reshape(2, rows // 2, size, heads, HD)
        .transpose(2, 3, 1, 0, 4)
        .reshape(size, heads, rows // 2, 2 * HD)
    )

    ffn_a = lax.psum_scatter(grad_down_t, dp, scatter_dimension=0, tiled=True)
    ffn_b = lax.psum_scatter(
        jnp.concatenate([grad_up_w, grad_out_t], axis=1), dp, scatter_dimension=0, tiled=True
    )
    ffn_a = lax.psum_scatter(ffn_a.reshape(shard, size, local_hidden).transpose(1, 0, 2), "tensor", scatter_dimension=0, tiled=False)
    ffn_b = jnp.concatenate(
        [
            ffn_b[:, : size * local_hidden].reshape(shard, size, local_hidden),
            ffn_b[:, size * local_hidden :].reshape(shard, size, local_width),
        ],
        axis=2,
    ).transpose(1, 0, 2)
    ffn_b = lax.psum_scatter(ffn_b, "tensor", scatter_dimension=0, tiled=False)
    grad_down_weight = ffn_a.astype(F32).T
    grad_up_weight = ffn_b[:, :local_hidden].astype(F32)
    grad_out_weight = ffn_b[:, local_hidden:].astype(F32).T

    qkv_all = lax.all_gather(
        jnp.concatenate([query_weight, key_weight, value_weight], axis=1), everyone, axis=0, tiled=True
    ).reshape(dp_size, size, shard, 3, heads, HD)
    qkv_all = jnp.concatenate([qkv_all, qkv_all], axis=1)
    qkv_all = lax.dynamic_slice_in_dim(qkv_all, rank, size, 1)

    total = grad_summed
    weight_grads, bias_grads = [], []
    for h in range(heads):
        arrived = exchange([grad_packed[k, h] for k in range(size)], size, 1)
        grads = attend_back(size, h, order, seg, slots[h], jnp.stack(arrived))
        grad_qv = grads[:, :rows].reshape(size * rows, CL)
        grad_k = grads[:, rows:].reshape(size, rows // 2, 2, HD).transpose(0, 2, 1, 3).reshape(size * rows, HD)
        tokens_h = jnp.concatenate([grad_qv, grad_k], axis=1)
        weight_grads.append(tn(x_all, tokens_h).astype(BF16))
        bias_grads.append(jnp.sum(grad_qv.astype(F32), axis=0))
        back = exchange([grads[k] for k in range(size)], size, -1)
        own_qv = jnp.stack([b[:rows] for b in back])
        own_k = jnp.stack([b[rows:] for b in back]).reshape(size, rows // 2, 2, HD).transpose(0, 2, 1, 3).reshape(size, rows, HD)
        full = jnp.concatenate([own_qv, own_k], axis=2).transpose(1, 0, 2).reshape(rows, size * 3 * HD)
        mat = jnp.concatenate([qkv_all[:, :, :, 0, h], qkv_all[:, :, :, 2, h], qkv_all[:, :, :, 1, h]], axis=-1)
        mat = mat.transpose(0, 2, 1, 3).reshape(width, size * 3 * HD)
        total = total + nt(full, mat)
    grad_inputs = total
    wg = lax.psum_scatter(jnp.concatenate(weight_grads, axis=1), dp, scatter_dimension=0, tiled=True)
    wg = wg.astype(F32).reshape(shard, heads, 3, HD)
    grad_query_weight = wg[:, :, 0].reshape(shard, local_width)
    grad_value_weight = wg[:, :, 1].reshape(shard, local_width)
    grad_key_weight = wg[:, :, 2].reshape(shard, local_width)

    bias = jnp.stack(bias_grads)
    bias = lax.psum(bias, dp)
    grad_query_bias = bias[:, :HD].reshape(local_width)
    grad_value_bias = bias[:, HD:].reshape(local_width)

    small = lax.psum(
        jnp.concatenate(
            [
                jnp.sum(grad_summed, axis=0),
                jnp.sum(grad_normed * hat1, axis=0),
                jnp.sum(grad_normed, axis=0),
                jnp.sum(grad_pre, axis=0),
                jnp.sum(cot * hat2, axis=0),
                jnp.sum(cot, axis=0),
                jnp.sum(grad_up.astype(F32), axis=0),
            ]
        ),
        everyone,
    )
    vec = [small[i * width : (i + 1) * width] for i in range(6)]
    grad_up_bias = lax.dynamic_slice_in_dim(small, 6 * width + rank * local_hidden, local_hidden, 0)
    return (
        layer_out, grad_inputs, grad_query_weight, grad_query_bias, grad_key_weight, grad_value_weight,
        grad_value_bias, grad_out_weight, vec[0], vec[1], vec[2], grad_up_weight, grad_up_bias,
        grad_down_weight, vec[3], vec[4], vec[5],
    )


def solution(mesh):
    devices = mesh.devices
    split = Mesh(devices.reshape(devices.shape[0] // 2, 2, devices.shape[1]), ("chip", "core", "tensor"))
    dp = ("chip", "core")
    rows, weight, turned, vector, same = (
        P(dp + ("tensor",), None),
        P(dp, "tensor"),
        P("tensor", dp),
        P("tensor"),
        P(),
    )
    in_specs = (
        rows, rows, P(dp, None), P(dp, None), P(dp, "tensor", None), weight, vector, weight, weight,
        vector, turned, same, same, same, weight, vector, turned, same, same, same,
    )
    out_specs = (
        rows, rows, weight, vector, weight, weight, vector, turned, same, same, same, weight, vector,
        turned, same, same, same,
    )
    return jax.shard_map(local, mesh=split, in_specs=in_specs, out_specs=out_specs, check_vma=False)
```

time: 1210 us -> 618 us (0.51)
  waiting for transfers between devices: 573 us -> 88.3 us
  local copies, waits for them, and re-layouts: 417 us -> 127 us
  Pallas kernels: 0 us -> 92.6 us
  starting transfers between devices: 1.95 us -> 58.8 us
  blocking collectives: 85.3 us -> 134 us
  matrix products: 85.4 us -> 45.4 us
  other arithmetic: 23.4 us -> 46.5 us
    gather x22 -> x0, local copies, waits for them, and re-layouts: 365 us -> none  [the longest x9 164 us: to_slots(): picked = jnp.take_along_axis(per_head, slot_order[:, :, None], axis=1)]
    reduce_scatter x6 -> x4, waiting for transfers between devices: 251 us -> 24.4 us  [the longest x1 22.4 us: local(): ffn_b = lax.psum_scatter(ffn_b, 'tensor', scatter_dimension=0, tiled=False)]
    all_gather x6 -> x2, waiting for transfers between devices: 204 us -> 0.04 us  [the longest x1 0.02 us: local(): lax.all_gather(jnp.concatenate([up_weight, down_weight.T, out_weight.T],...]
    unnamed x20 -> x8, waiting for transfers between devices: 118 us -> 0.12 us
    pallas_call x0 -> x7, Pallas kernels: none -> 92.6 us  [the longest x3 43.7 us: attend_back(): pl.pallas_call(functools.partial(backward_kernel, blocks), grid=(1,), in_...]
    ppermute x0 -> x33, waiting for transfers between devices: none -> 63.7 us  [the longest x3 23.1 us: gather_line(): lax.ppermute(up, 'tensor', [(i, i + 1) for i in range(k - 1, size - 1)])]
    ppermute x0 -> x33, starting transfers between devices: none -> 58.6 us  [the longest x27 46.6 us: exchange(): lax.ppermute(parts[k], 'tensor', [(i, (i + sign * k) % size) for i in ran...]
    all_gather x4 -> x2, blocking collectives: 42.2 us -> 82.4 us  [the longest x1 66.5 us: local(): up_bias_full = lax.all_gather(up_bias, 'tensor', axis=0, tiled=True)]
  transfers between devices with their start and end apart: 16 -> 40, of which waited for: 12 -> 12; matrix products, arithmetic and copies ran while one was open for 21% -> 34% of each run, Pallas kernels for 0% -> 15%
where the time goes in v1:
time: 618 us; the launch traced here: 608 us
  blocking collectives  134 us (22%)
  local copies, waits for them, and re-layouts  127 us (21%)
  Pallas kernels  92.6 us (15%)
  waiting for transfers between devices  88.3 us (14%)
  starting transfers between devices  58.8 us (10%)
  other arithmetic  46.5 us (8%)
  matrix products  45.4 us (7%)
  between operations  16.1 us (3%)
    all_gather x1, blocking collectives, local(): up_bias_full = lax.all_gather(up_bias, 'tensor', axis=0, tiled=True)  66.5 us
    ppermute x27, starting transfers between devices, exchange(): lax.ppermute(parts[k], 'tensor', [(i, (i + sign * k) % size) for i in ran...  46.6 us
    pallas_call x3, Pallas kernels, attend_back(): pl.pallas_call(functools.partial(backward_kernel, blocks), grid=(1,), in_...  43.7 us
    pallas_call x3, Pallas kernels, attend(): pl.pallas_call(functools.partial(forward_kernel, blocks), grid=(1,), in_s...  41.1 us
    psum x1, blocking collectives, local(): lax.psum(jnp.concatenate([jnp.sum(grad_summed, axis=0), jnp.sum(grad_norm...  39.5 us
    unnamed x126, local copies, waits for them, and re-layouts  35.1 us
    ppermute x3, waiting for transfers between devices, gather_line(): lax.ppermute(up, 'tensor', [(i, i + 1) for i in range(k - 1, size - 1)])  23.1 us
    reduce_scatter x1, waiting for transfers between devices, local(): ffn_b = lax.psum_scatter(ffn_b, 'tensor', scatter_dimension=0, tiled=False)  22.4 us
  transfers between devices with their start and end apart: 40, of which 12 were waited for; matrix products, arithmetic and copies ran while one was open for 34% of the time, Pallas kernels for 15%

profile of v1, /device:TPU:0, one launch (start us, length us, event | category | flops | bytes accessed | tf_op | source)
XLA Modules:
  0.0 608.0 jit_solution(11998519702362669331)
XLA Ops:
  8.2 1.7 pad_maximum_fusion.3
  10.0 5.0 collective-permute-start
  16.3 23.1 %collective-permute-done = bf16[512,768]{1,0:T(8,128)(2,1)S(1)} collective-permute-done((bf16[512,768]{1,0:T(8,128)(2,1)}, bf16[512,768]{1,0:T(8,128)(2,1)S(1)}, u32[]{:S(2)}, u32[]{:S(2)}) %collective-permute-start) | collective-permute-done | bytes 786464 | tf_op jit(solution)/shard_map/ppermute | solution.py:279
  44.8 15.9 %all_gather.12 = bf16[768,576]{1,0:T(8,128)(2,1)S(1)} all-gather(bf16[96,576]{1,0:T(8,128)(2,1)} %pad_maximum_fusion.8), channel_id=1, replica_groups=mesh['chip'=4,'core'=2,'tensor'=4] {'chip','core'}, dimensions={0}, use_global_device_ids=true | all-gather | bytes 995328 | tf_op jit(solution)/shard_map/all_gather | solution.py:307
  64.6 66.5 %all-gather = f32[4,1,768]{2,1,0:T(1,128)S(1)} all-gather(f32[1,1,768]{2,1,0:T(1,128)S(1)} %reshape.330), channel_id=1, replica_groups=mesh['chip'=4,'core'=2,'tensor'=4] {'tensor'}, dimensions={0}, use_global_device_ids=true | all-gather | bytes 15360 | tf_op jit(solution)/shard_map/all_gather | solution.py:328
  131.2 7.8 %slot_tokens.1 = (f32[3,1,2048]{2,1,0:T(1,128)S(1)}, f32[3,1,2048]{2,1,0:T(1,128)S(1)}) custom-call(s32[5]{0:T(128)S(1)} %pad_add_fusion.scal_ref, s32[3,1,2048]{2,1,0:T(1,128)S(1)} %bitcast.256, s32[1,2048]{1,0:T(1,128)S(1)} %copy-done.6), custom_call_target="tpu_custom_call" | custom-call | flops 201326592 | bytes 98304 | tf_op jit(solution)/shard_map/slot_tokens/pallas_call | solution.py:188
  143.7 20.8 %collective-permute-done.3 = bf16[512,768]{1,0:T(8,128)(2,1)S(1)} collective-permute-done((bf16[512,768]{1,0:T(8,128)(2,1)}, bf16[512,768]{1,0:T(8,128)(2,1)S(1)}, u32[]{:S(2)}, u32[]{:S(2)}) %collective-permute-start.3) | collective-permute-done | bytes 786464 | tf_op jit(solution)/shard_map/ppermute | solution.py:280
  165.0 13.7 %attend.3 = (bf16[1,2048,256]{2,1,0:T(8,128)(2,1)S(1)}, bf16[4,256,128]{2,1,0:T(8,128)(2,1)S(1)}) custom-call(f32[3,1,2048]{2,1,0:T(1,128)S(1)} %get-tuple-element.25.order_ref, f32[3,1,2048]{2,1,0:T(1,128)S(1)} %get-tuple-element.26.seg_ref, bf16[2048,768]{1,0:T(8,128)(2,1)S(1)} %pad_maximum_fusion.1.x_ref, ...), custom_call_target="tpu_custom_call" | custom-call | flops 4026531840 | bytes 4718592 | tf_op jit(solution)/shard_map/attend/pallas_call | solution.py:208
  178.7 13.7 %attend.4 = (bf16[1,2048,256]{2,1,0:T(8,128)(2,1)S(1)}, bf16[4,256,128]{2,1,0:T(8,128)(2,1)S(1)}) custom-call(f32[3,1,2048]{2,1,0:T(1,128)S(1)} %get-tuple-element.25.order_ref, f32[3,1,2048]{2,1,0:T(1,128)S(1)} %get-tuple-element.26.seg_ref, bf16[2048,768]{1,0:T(8,128)(2,1)S(1)} %pad_maximum_fusion.1.x_ref, ...), custom_call_target="tpu_custom_call" | custom-call | flops 4026531840 | bytes 4718592 | tf_op jit(solution)/shard_map/attend/pallas_call | solution.py:208
  192.8 3.4 collective-permute-start.9
  196.3 13.7 %attend.5 = (bf16[1,2048,256]{2,1,0:T(8,128)(2,1)S(1)}, bf16[4,256,128]{2,1,0:T(8,128)(2,1)S(1)}) custom-call(f32[3,1,2048]{2,1,0:T(1,128)S(1)} %get-tuple-element.25.order_ref, f32[3,1,2048]{2,1,0:T(1,128)S(1)} %get-tuple-element.26.seg_ref, bf16[2048,768]{1,0:T(8,128)(2,1)S(1)} %pad_maximum_fusion.1.x_ref, ...), custom_call_target="tpu_custom_call" | custom-call | flops 4026531840 | bytes 4718592 | tf_op jit(solution)/shard_map/attend/pallas_call | solution.py:208
  213.1 2.0 collective-permute-start.13
  215.1 1.9 collective-permute-start.8
  220.1 3.2 collective-permute-done.11
  227.3 2.7 slice.390
  230.0 2.9 copy.308
  232.9 4.2 reshape.295
  237.1 6.7 %fusion.35 = (bf16[8,4,96,768]{3,2,1,0:T(8,128)(2,1)}, bf16[8,4,96,768]{3,2,1,0:T(8,128)(2,1)S(1)}) fusion(bf16[8,4,96,1728]{3,2,1,0:T(8,128)(2,1)} %bitcast.260), kind=kLoop, calls=%fused_computation.152 | loop fusion | bytes 18874368 | tf_op jit(solution)/shard_map/slice | solution.py:323
  243.8 6.0 copy.309
  250.8 3.6 copy.310
  257.3 2.9 fusion.30
  260.3 4.2 fusion.45
  267.0 2.1 fusion.32
  270.4 4.7 convolution_convert_fusion
  275.1 9.7 %convert_reduce_fusion = (f32[3072]{0:T(1024)}, bf16[512,3072]{1,0:T(8,128)(2,1)S(1)}) fusion(f32[512,3072]{1,0:T(8,128)} %copy-done.45, f32[3072]{0:T(1024)S(1)} %bitcast.341, bf16[768,3072]{1,0:T(8,128)(2,1)} %bitcast.265, f32[512,768]{1,0:T(8,128)} %copy-done.19), kind=kOutput, calls=%fused_computation.5 | convolution fusion | flops 2449339392 | bytes 15753216 | tf_op jit(solution)/shard_map/dot_general | solution.py:19
  284.8 6.6 %multiply_reduce_fusion = (f32[768]{0:T(1024)}, f32[512]{0:T(512)S(1)}, f32[512]{0:T(512)S(1)}, f32[768]{0:T(1024)}, f32[512,768]{1,0:T(8,128)S(1)}) fusion(f32[512,768]{1,0:T(8,128)S(1)} %copy-done.12, f32[512]{0:T(512)S(1)} %add_rsqrt_fusion.1, f32[512]{0:T(512)S(1)} %broadcast_multiply_fusion.5, f32[768]{0:T(1024)S(1)} %copy-done.36, ...), kind=kOutput, calls=%fused_computation.30 | convolution fusion | flops 2419848704 | bytes 12600320 | tf_op jit(solution)/shard_map/dot_general | solution.py:23
  294.5 3.4 convolution_convert_fusion.1
  297.9 2.9 pad_maximum_fusion
  300.9 6.0 copy.246
  306.9 10.2 %reshape.303 = bf16[8,4,96,3,3,64]{2,1,0,5,4,3:T(4,128)(2,1)} reshape(bf16[3072,576]{0,1:T(8,128)(2,1)} %copy.246) | data formatting | bytes 7077888 | tf_op jit(solution)/shard_map/reshape | solution.py:401
  317.2 14.5 %fusion.2 = bf16[8,4,96,3,3,64]{2,1,0,5,4,3:T(4,128)(2,1)S(1)} fusion(s32[]{:T(128)S(6)} %select_n.45, bf16[8,4,96,3,3,64]{2,1,0,5,4,3:T(4,128)(2,1)} %reshape.303), kind=kLoop, calls=%fused_computation.11 | loop fusion | flops 7077888 | bytes 7077892 | tf_op jit(solution)/shard_map/concatenate | solution.py:402
  331.7 2.5 slice_bitcast_fusion.2
  334.2 3.7 maximum_bitcast_fusion
  339.2 3.9 reshape.304
  343.2 3.0 copy.262
  346.2 3.9 reshape.307
  350.1 2.3 maximum_bitcast_fusion.2
  353.8 3.9 reshape.310
  357.7 3.5 convolution_convert_fusion.3
  363.8 2.2 reshape.299
  367.1 1.9 collective-permute-start.28
  369.1 2.5 collective-permute-start.15
  372.0 2.4 collective-permute-start.17
  379.3 39.5 %psum.15 = f32[7680]{0:T(1024)S(1)} all-reduce(f32[7680]{0:T(1024)S(1)} %constant_dynamic-update-slice_fusion), channel_id=1, replica_groups=mesh['chip'=4,'core'=2,'tensor'=4] {'chip','core','tensor'}, use_global_device_ids=true, to_apply=%region_23.24 | all-reduce | flops 7680 | bytes 61440 | tf_op jit(solution)/shard_map/psum | solution.py:434
  420.9 2.3 collective-permute-start.21
  423.9 2.8 collective-permute-start.23
  428.0 1.9 collective-permute-done.22
  430.0 14.7 %attend_back.3 = bf16[4,768,128]{2,1,0:T(8,128)(2,1)S(1)} custom-call(f32[3,1,2048]{2,1,0:T(1,128)S(1)} %get-tuple-element.25.order_ref, f32[3,1,2048]{2,1,0:T(1,128)S(1)} %get-tuple-element.26.seg_ref, bf16[1,2048,256]{2,1,0:T(8,128)(2,1)S(1)} %get-tuple-element.30.slots_ref, bf16[4,256,128]{2,1,0:T(8,128)(2,1)S(1)} %pad_maximum_fusion.4.g_ref), custom_call_target="tpu_custom_call" | custom-call | flops 3221225472 | bytes 3145728 | tf_op jit(solution)/shard_map/attend_back/pallas_call | solution.py:235
  444.7 14.5 %attend_back.4 = bf16[4,768,128]{2,1,0:T(8,128)(2,1)S(1)} custom-call(f32[3,1,2048]{2,1,0:T(1,128)S(1)} %get-tuple-element.25.order_ref, f32[3,1,2048]{2,1,0:T(1,128)S(1)} %get-tuple-element.26.seg_ref, bf16[1,2048,256]{2,1,0:T(8,128)(2,1)S(1)} %get-tuple-element.31.slots_ref, bf16[4,256,128]{2,1,0:T(8,128)(2,1)S(1)} %pad_maximum_fusion.5.g_ref), custom_call_target="tpu_custom_call" | custom-call | flops 3221225472 | bytes 3145728 | tf_op jit(solution)/shard_map/attend_back/pallas_call | solution.py:235
  461.0 14.5 %attend_back.5 = bf16[4,768,128]{2,1,0:T(8,128)(2,1)S(1)} custom-call(f32[3,1,2048]{2,1,0:T(1,128)S(1)} %get-tuple-element.25.order_ref, f32[3,1,2048]{2,1,0:T(1,128)S(1)} %get-tuple-element.26.seg_ref, bf16[1,2048,256]{2,1,0:T(8,128)(2,1)S(1)} %copy-done.8, bf16[4,256,128]{2,1,0:T(8,128)(2,1)S(1)} %pad_maximum_fusion.6.g_ref), custom_call_target="tpu_custom_call" | custom-call | flops 3221225472 | bytes 3145728 | tf_op jit(solution)/shard_map/attend_back/pallas_call | solution.py:235
  477.7 11.8 %psum.14 = f32[3,128]{1,0:T(4,128)S(1)} all-reduce(f32[3,128]{1,0:T(4,128)S(1)} %pad_maximum_fusion.9), channel_id=1, replica_groups=mesh['chip'=4,'core'=2,'tensor'=4] {'chip','core'}, use_global_device_ids=true, to_apply=%region_13.14 | all-reduce | flops 384 | bytes 3072 | tf_op jit(solution)/shard_map/psum | solution.py:430
  495.3 2.9 collective-permute-start.30
  499.7 3.8 collective-permute-start.18
  504.8 2.0 convolution_convert_fusion.6
  509.6 4.7 collective-permute-start.20
  516.9 8.9 %collective-permute-done.31 = bf16[768,128]{1,0:T(8,128)(2,1)} collective-permute-done((bf16[768,128]{1,0:T(8,128)(2,1)}, bf16[768,128]{1,0:T(8,128)(2,1)}, u32[]{:S(2)}, u32[]{:S(2)}) %collective-permute-start.31) | collective-permute-done | bytes 196640 | tf_op jit(solution)/shard_map/ppermute | solution.py:270
  529.4 9.6 %collective-permute-start.26 = (bf16[768,128]{1,0:T(8,128)(2,1)}, bf16[768,128]{1,0:T(8,128)(2,1)}, u32[]{:S(2)}, u32[]{:S(2)}) collective-permute-start(bf16[768,128]{1,0:T(8,128)(2,1)} %get-tuple-element.147), channel_id=1, source_target_pairs={{0,1},{1,2},{2,3},{3,0},{4,5},{5,6},{6,7},{7,4},{8,9},{9,10},{10,1... | collective-permute-start | bytes 589832 | tf_op jit(solution)/shard_map/ppermute | solution.py:270
  540.0 2.7 collective-permute-done.19
  548.5 2.0 copy.329
  562.3 2.1 fusion.46
  566.2 2.0 add_add_fusion
  571.5 1.9 reduce-scatter.14.cloned.1.call-done
  573.5 1.6 convert_bitcast_fusion
  575.1 22.4 %reduce-scatter.10.cloned.1.call-done = bf16[1,96,960]{2,1,0:T(8,128)(2,1)} async-done(((bf16[4,96,960]{2,1,0:T(8,128)(2,1)}), bf16[1,96,960]{2,1,0:T(8,128)(2,1)}) %reduce-scatter.10.cloned.1.call-update) | async-done | bytes 184336 | tf_op jit(solution)/shard_map/reduce_scatter | solution.py:394
  (338 shorter events, 101.7 us)
Async XLA Ops:
  7.2 220.2 %all-gather.4.cloned.1.call-start = ((), (), s32[]{:S(2)}) async-start(), calls=%async_computation.5 | async-start | bytes 11354112 | tf_op jit(solution)/shard_map/all_gather | solution.py:318
  8.1 53.2 %copy-start.39 = (f32[192]{0:T(256)S(1)}, f32[192]{0:T(256)}, u32[]{:S(2)}) copy-start(f32[192]{0:T(256)} %param.26) | copy-start | bytes 2308
  8.1 53.3 %copy-start.40 = (f32[192]{0:T(256)S(1)}, f32[192]{0:T(256)}, u32[]{:S(2)}) copy-start(f32[192]{0:T(256)} %param.29) | copy-start | bytes 2308
  9.9 291.0 %all-gather.6.cloned.1.call-start = ((), (), s32[]{:S(2)}) async-start(), calls=%async_computation.6 | async-start | bytes 4055040 | tf_op jit(solution)/shard_map/all_gather | solution.py:399
  10.0 29.4 %collective-permute-start = (bf16[512,768]{1,0:T(8,128)(2,1)}, bf16[512,768]{1,0:T(8,128)(2,1)S(1)}, u32[]{:S(2)}, u32[]{:S(2)}) collective-permute-start(bf16[512,768]{1,0:T(8,128)(2,1)} %param.20), channel_id=1, source_target_pairs={{0,1},{1,2},{2,3},{4,5},{5,6},{6,7},{8,9},{9,10},{10,11},{12,13},{... | collective-permute-start | bytes 2359304 | tf_op jit(solution)/shard_map/ppermute | solution.py:279
  15.0 28.6 %collective-permute-start.1 = (bf16[512,768]{1,0:T(8,128)(2,1)}, bf16[512,768]{1,0:T(8,128)(2,1)}, u32[]{:S(2)}, u32[]{:S(2)}) collective-permute-start(bf16[512,768]{1,0:T(8,128)(2,1)} %param.20), channel_id=1, source_target_pairs={{1,0},{2,1},{3,2},{5,4},{6,5},{7,6},{9,8},{10,9},{11,10},{13,12},{... | collective-permute-start | bytes 2359304 | tf_op jit(solution)/shard_map/ppermute | solution.py:280
  39.4 22.2 %collective-permute-start.4 = (bf16[512,768]{1,0:T(8,128)(2,1)S(1)}, bf16[512,768]{1,0:T(8,128)(2,1)}, u32[]{:S(2)}, u32[]{:S(2)}) collective-permute-start(bf16[512,768]{1,0:T(8,128)(2,1)S(1)} %collective-permute-done), channel_id=1, source_target_pairs={{1,2},{2,3},{5,6},{6,7},{9,10},{10,11},{13,14},{14,15},{17,18},{18... | collective-permute-start | bytes 2359304 | tf_op jit(solution)/shard_map/ppermute | solution.py:279
  42.5 506.0 %reduce-scatter.12.cloned.1.call-start = ((), (), s32[]{:S(2)}) async-start(), calls=%async_computation.9 | async-start | bytes 5308416 | tf_op jit(solution)/shard_map/reduce_scatter | solution.py:382
  43.5 95.5 %collective-permute-start.2 = (bf16[512,768]{1,0:T(8,128)(2,1)}, bf16[512,768]{1,0:T(8,128)(2,1)}, u32[]{:S(2)}, u32[]{:S(2)}) collective-permute-start(bf16[512,768]{1,0:T(8,128)(2,1)} %collective-permute-done.1), channel_id=1, source_target_pairs={{1,0},{2,1},{5,4},{6,5},{9,8},{10,9},{13,12},{14,13},{17,16},{18,1... | collective-permute-start | bytes 2359304 | tf_op jit(solution)/shard_map/ppermute | solution.py:280
  61.5 69.7 %copy-start.5 = (s32[1,3,2048]{2,0,1:T(1,128)S(1)}, s32[1,3,2048]{2,0,1:T(1,128)}, u32[]{:S(2)}) copy-start(s32[1,3,2048]{2,0,1:T(1,128)} %param.24) | copy-start | bytes 73732
  61.5 69.7 %copy-start.6 = (s32[1,2048]{1,0:T(1,128)S(1)}, s32[1,2048]{1,0:T(1,128)}, u32[]{:S(2)}) copy-start(s32[1,2048]{1,0:T(1,128)} %balance_ref.1) | copy-start | bytes 24580
  61.6 80.8 %collective-permute-start.5 = (bf16[512,768]{1,0:T(8,128)(2,1)}, bf16[512,768]{1,0:T(8,128)(2,1)}, u32[]{:S(2)}, u32[]{:S(2)}) collective-permute-start(bf16[512,768]{1,0:T(8,128)(2,1)} %collective-permute-done.4), channel_id=1, source_target_pairs={{2,3},{6,7},{10,11},{14,15},{18,19},{22,23},{26,27},{30,31}} | collective-permute-start | bytes 2359304 | tf_op jit(solution)/shard_map/ppermute | solution.py:279
  139.1 25.4 %collective-permute-start.3 = (bf16[512,768]{1,0:T(8,128)(2,1)}, bf16[512,768]{1,0:T(8,128)(2,1)S(1)}, u32[]{:S(2)}, u32[]{:S(2)}) collective-permute-start(bf16[512,768]{1,0:T(8,128)(2,1)} %collective-permute-done.2), channel_id=1, source_target_pairs={{1,0},{5,4},{9,8},{13,12},{17,16},{21,20},{25,24},{29,28}} | collective-permute-start | bytes 2359304 | tf_op jit(solution)/shard_map/ppermute | solution.py:280
  142.4 22.2 %copy-start.24 = (bf16[512,768]{1,0:T(8,128)(2,1)S(1)}, bf16[512,768]{1,0:T(8,128)(2,1)}, u32[]{:S(2)}) copy-start(bf16[512,768]{1,0:T(8,128)(2,1)} %param.20) | copy-start | bytes 2359300
  165.0 31.3 %copy-start.3 = (bf16[2048,768]{1,0:T(8,128)(2,1)}, bf16[2048,768]{1,0:T(8,128)(2,1)S(1)}, u32[]{:S(2)}) copy-start(bf16[2048,768]{1,0:T(8,128)(2,1)S(1)} %pad_maximum_fusion.1.x_ref) | copy-start | bytes 9437188
  192.5 20.6 %collective-permute-start.6 = (bf16[256,128]{1,0:T(8,128)(2,1)S(1)}, bf16[256,128]{1,0:T(8,128)(2,1)S(1)}, u32[]{:S(2)}, u32[]{:S(2)}) collective-permute-start(bf16[256,128]{1,0:T(8,128)(2,1)S(1)} %get-tuple-element.152), channel_id=1, source_target_pairs={{0,3},{1,0},{2,1},{3,2},{4,7},{5,4},{6,5},{7,6},{8,11},{9,8},{10,9... | collective-permute-start | bytes 196616 | tf_op jit(solution)/shard_map/ppermute | solution.py:270
  192.6 22.5 %collective-permute-start.7 = (bf16[256,128]{1,0:T(8,128)(2,1)S(1)}, bf16[256,128]{1,0:T(8,128)(2,1)S(1)}, u32[]{:S(2)}, u32[]{:S(2)}) collective-permute-start(bf16[256,128]{1,0:T(8,128)(2,1)S(1)} %get-tuple-element.180), channel_id=1, source_target_pairs={{0,3},{1,0},{2,1},{3,2},{4,7},{5,4},{6,5},{7,6},{8,11},{9,8},{10,9... | collective-permute-start | bytes 196616 | tf_op jit(solution)/shard_map/ppermute | solution.py:270
  192.8 24.1 %collective-permute-start.9 = (bf16[256,128]{1,0:T(8,128)(2,1)S(1)}, bf16[256,128]{1,0:T(8,128)(2,1)S(1)}, u32[]{:S(2)}, u32[]{:S(2)}) collective-permute-start(bf16[256,128]{1,0:T(8,128)(2,1)S(1)} %get-tuple-element.151), channel_id=1, source_target_pairs={{0,2},{1,3},{2,0},{3,1},{4,6},{5,7},{6,4},{7,5},{8,10},{9,11},{10,... | collective-permute-start | bytes 196616 | tf_op jit(solution)/shard_map/ppermute | solution.py:270
  196.2 20.7 %collective-permute-start.10 = (bf16[256,128]{1,0:T(8,128)(2,1)S(1)}, bf16[256,128]{1,0:T(8,128)(2,1)S(1)}, u32[]{:S(2)}, u32[]{:S(2)}) collective-permute-start(bf16[256,128]{1,0:T(8,128)(2,1)S(1)} %get-tuple-element.181), channel_id=1, source_target_pairs={{0,2},{1,3},{2,0},{3,1},{4,6},{5,7},{6,4},{7,5},{8,10},{9,11},{10,... | collective-permute-start | bytes 196616 | tf_op jit(solution)/shard_map/ppermute | solution.py:270
  211.6 7.1 %collective-permute-start.12 = (bf16[256,128]{1,0:T(8,128)(2,1)S(1)}, bf16[256,128]{1,0:T(8,128)(2,1)S(1)}, u32[]{:S(2)}, u32[]{:S(2)}) collective-permute-start(bf16[256,128]{1,0:T(8,128)(2,1)S(1)} %get-tuple-element.150), channel_id=1, source_target_pairs={{0,1},{1,2},{2,3},{3,0},{4,5},{5,6},{6,7},{7,4},{8,9},{9,10},{10,1... | collective-permute-start | bytes 196616 | tf_op jit(solution)/shard_map/ppermute | solution.py:270
  213.1 6.2 %collective-permute-start.13 = (bf16[256,128]{1,0:T(8,128)(2,1)S(1)}, bf16[256,128]{1,0:T(8,128)(2,1)S(1)}, u32[]{:S(2)}, u32[]{:S(2)}) collective-permute-start(bf16[256,128]{1,0:T(8,128)(2,1)S(1)} %get-tuple-element.182), channel_id=1, source_target_pairs={{0,1},{1,2},{2,3},{3,0},{4,5},{5,6},{6,7},{7,4},{8,9},{9,10},{10,1... | collective-permute-start | bytes 196616 | tf_op jit(solution)/shard_map/ppermute | solution.py:270
  215.1 4.9 collective-permute-start.8
  217.0 6.4 %collective-permute-start.11 = (bf16[256,128]{1,0:T(8,128)(2,1)}, bf16[256,128]{1,0:T(8,128)(2,1)S(1)}, u32[]{:S(2)}, u32[]{:S(2)}) collective-permute-start(bf16[256,128]{1,0:T(8,128)(2,1)} %get-tuple-element.159), channel_id=1, source_target_pairs={{0,2},{1,3},{2,0},{3,1},{4,6},{5,7},{6,4},{7,5},{8,10},{9,11},{10,... | collective-permute-start | bytes 196616 | tf_op jit(solution)/shard_map/ppermute | solution.py:270
  217.0 6.5 %collective-permute-start.14 = (bf16[256,128]{1,0:T(8,128)(2,1)S(1)}, bf16[256,128]{1,0:T(8,128)(2,1)S(1)}, u32[]{:S(2)}, u32[]{:S(2)}) collective-permute-start(bf16[256,128]{1,0:T(8,128)(2,1)S(1)} %get-tuple-element.158), channel_id=1, source_target_pairs={{0,1},{1,2},{2,3},{3,0},{4,5},{5,6},{6,7},{7,4},{8,9},{9,10},{10,1... | collective-permute-start | bytes 196616 | tf_op jit(solution)/shard_map/ppermute | solution.py:270
  250.8 6.4 %copy-start.13 = (bf16[96,8,4,768]{3,1,2,0:T(8,128)(2,1)}, bf16[96,8,4,768]{3,1,2,0:T(8,128)(2,1)S(1)}, u32[]{:S(2)}) copy-start(bf16[96,8,4,768]{3,1,2,0:T(8,128)(2,1)S(1)} %copy.325) | copy-start | bytes 14155780
  255.6 4.7 copy-start.14
  256.9 3.3 copy-start.11
  260.2 8.9 %copy-start.45 = (f32[512,3072]{1,0:T(8,128)}, f32[512,3072]{1,0:T(8,128)S(1)}, u32[]{:S(2)}) copy-start(f32[512,3072]{1,0:T(8,128)S(1)} %fusion.30) | copy-start | bytes 18874372
  260.3 4.6 copy-start.35
  275.0 284.8 %reduce-scatter.8.cloned.1.call-start = ((), (), s32[]{:S(2)}) async-start(), calls=%async_computation.7 | async-start | bytes 6635520 | tf_op jit(solution)/shard_map/reduce_scatter | solution.py:383
  275.1 9.7 %copy-start.12 = (f32[512,768]{1,0:T(8,128)S(1)}, f32[512,768]{1,0:T(8,128)}, u32[]{:S(2)}) copy-start(f32[512,768]{1,0:T(8,128)} %copy-done.11) | copy-start | bytes 4718596
  275.1 9.7 %copy-start.20 = (f32[512,768]{1,0:T(8,128)S(1)}, f32[512,768]{1,0:T(8,128)}, u32[]{:S(2)}) copy-start(f32[512,768]{1,0:T(8,128)} %copy-done.19) | copy-start | bytes 4718596
  300.8 267.4 %reduce-scatter.16.cloned.1.call-start = ((), (), s32[]{:S(2)}) async-start(), calls=%async_computation.11 | async-start | bytes 1105920
  346.1 3.9 copy-start.17
  346.2 3.9 copy-start.18
  366.3 93.7 %collective-permute-start.27 = (bf16[256,128]{1,0:T(8,128)(2,1)S(1)}, bf16[256,128]{1,0:T(8,128)(2,1)}, u32[]{:S(2)}, u32[]{:S(2)}) collective-permute-start(bf16[256,128]{1,0:T(8,128)(2,1)S(1)} %bitcast.325), channel_id=1, source_target_pairs={{0,1},{1,2},{2,3},{3,0},{4,5},{5,6},{6,7},{7,4},{8,9},{9,10},{10,1... | collective-permute-start | bytes 196616 | tf_op jit(solution)/shard_map/ppermute | solution.py:270
  367.1 93.0 %collective-permute-start.28 = (bf16[256,128]{1,0:T(8,128)(2,1)}, bf16[256,128]{1,0:T(8,128)(2,1)}, u32[]{:S(2)}, u32[]{:S(2)}) collective-permute-start(bf16[256,128]{1,0:T(8,128)(2,1)} %bitcast.93), channel_id=1, source_target_pairs={{0,2},{1,3},{2,0},{3,1},{4,6},{5,7},{6,4},{7,5},{8,10},{9,11},{10,... | collective-permute-start | bytes 196616 | tf_op jit(solution)/shard_map/ppermute | solution.py:270
  369.1 51.8 %collective-permute-start.15 = (bf16[256,128]{1,0:T(8,128)(2,1)S(1)}, bf16[256,128]{1,0:T(8,128)(2,1)S(1)}, u32[]{:S(2)}, u32[]{:S(2)}) collective-permute-start(bf16[256,128]{1,0:T(8,128)(2,1)S(1)} %bitcast.328), channel_id=1, source_target_pairs={{0,1},{1,2},{2,3},{3,0},{4,5},{5,6},{6,7},{7,4},{8,9},{9,10},{10,1... | collective-permute-start | bytes 196616 | tf_op jit(solution)/shard_map/ppermute | solution.py:270
  371.8 51.5 %collective-permute-start.16 = (bf16[256,128]{1,0:T(8,128)(2,1)S(1)}, bf16[256,128]{1,0:T(8,128)(2,1)S(1)}, u32[]{:S(2)}, u32[]{:S(2)}) collective-permute-start(bf16[256,128]{1,0:T(8,128)(2,1)S(1)} %bitcast.327), channel_id=1, source_target_pairs={{0,2},{1,3},{2,0},{3,1},{4,6},{5,7},{6,4},{7,5},{8,10},{9,11},{10,... | collective-permute-start | bytes 196616 | tf_op jit(solution)/shard_map/ppermute | solution.py:270
  372.0 51.9 %collective-permute-start.17 = (bf16[256,128]{1,0:T(8,128)(2,1)S(1)}, bf16[256,128]{1,0:T(8,128)(2,1)S(1)}, u32[]{:S(2)}, u32[]{:S(2)}) collective-permute-start(bf16[256,128]{1,0:T(8,128)(2,1)S(1)} %bitcast.326), channel_id=1, source_target_pairs={{0,3},{1,0},{2,1},{3,2},{4,7},{5,4},{6,5},{7,6},{8,11},{9,8},{10,9... | collective-permute-start | bytes 196616 | tf_op jit(solution)/shard_map/ppermute | solution.py:270
  420.9 6.9 %collective-permute-start.21 = (bf16[256,128]{1,0:T(8,128)(2,1)S(1)}, bf16[256,128]{1,0:T(8,128)(2,1)S(1)}, u32[]{:S(2)}, u32[]{:S(2)}) collective-permute-start(bf16[256,128]{1,0:T(8,128)(2,1)S(1)} %bitcast.331), channel_id=1, source_target_pairs={{0,1},{1,2},{2,3},{3,0},{4,5},{5,6},{6,7},{7,4},{8,9},{9,10},{10,1... | collective-permute-start | bytes 196616 | tf_op jit(solution)/shard_map/ppermute | solution.py:270
  423.3 6.7 %collective-permute-start.22 = (bf16[256,128]{1,0:T(8,128)(2,1)S(1)}, bf16[256,128]{1,0:T(8,128)(2,1)S(1)}, u32[]{:S(2)}, u32[]{:S(2)}) collective-permute-start(bf16[256,128]{1,0:T(8,128)(2,1)S(1)} %bitcast.330), channel_id=1, source_target_pairs={{0,2},{1,3},{2,0},{3,1},{4,6},{5,7},{6,4},{7,5},{8,10},{9,11},{10,... | collective-permute-start | bytes 196616 | tf_op jit(solution)/shard_map/ppermute | solution.py:270
  423.9 6.0 collective-permute-start.23
  427.8 32.3 %collective-permute-start.29 = (bf16[256,128]{1,0:T(8,128)(2,1)}, bf16[256,128]{1,0:T(8,128)(2,1)S(1)}, u32[]{:S(2)}, u32[]{:S(2)}) collective-permute-start(bf16[256,128]{1,0:T(8,128)(2,1)} %bitcast.95), channel_id=1, source_target_pairs={{0,3},{1,0},{2,1},{3,2},{4,7},{5,4},{6,5},{7,6},{8,11},{9,8},{10,9... | collective-permute-start | bytes 196616 | tf_op jit(solution)/shard_map/ppermute | solution.py:270
  459.2 44.8 %copy-start = (bf16[4,768,128]{2,1,0:T(8,128)(2,1)}, bf16[4,768,128]{2,1,0:T(8,128)(2,1)S(1)}, u32[]{:S(2)}) copy-start(bf16[4,768,128]{2,1,0:T(8,128)(2,1)S(1)} %attend_back.4) | copy-start | bytes 2359300
  475.5 15.5 %copy-start.1 = (bf16[4,768,128]{2,1,0:T(8,128)(2,1)}, bf16[4,768,128]{2,1,0:T(8,128)(2,1)S(1)}, u32[]{:S(2)}) copy-start(bf16[4,768,128]{2,1,0:T(8,128)(2,1)S(1)} %attend_back.5) | copy-start | bytes 2359300
  491.1 3.4 copy-start.2
  493.4 11.4 %copy-start.28 = (bf16[4,2,256,64]{3,2,1,0:T(8,128)(2,1)S(1)}, bf16[4,2,256,64]{3,2,1,0:T(8,128)(2,1)}, u32[]{:S(2)}) copy-start(bf16[4,2,256,64]{3,2,1,0:T(8,128)(2,1)} %copy.297) | copy-start | bytes 786436
  494.4 10.4 %copy-start.4 = (bf16[2048,768]{1,0:T(8,128)(2,1)S(1)}, bf16[2048,768]{1,0:T(8,128)(2,1)}, u32[]{:S(2)}) copy-start(bf16[2048,768]{1,0:T(8,128)(2,1)} %copy-done.3) | copy-start | bytes 9437188
  495.3 13.7 %collective-permute-start.30 = (bf16[768,128]{1,0:T(8,128)(2,1)S(1)}, bf16[768,128]{1,0:T(8,128)(2,1)S(1)}, u32[]{:S(2)}, u32[]{:S(2)}) collective-permute-start(bf16[768,128]{1,0:T(8,128)(2,1)S(1)} %get-tuple-element.128), channel_id=1, source_target_pairs={{0,3},{1,0},{2,1},{3,2},{4,7},{5,4},{6,5},{7,6},{8,11},{9,8},{10,9... | collective-permute-start | bytes 589832 | tf_op jit(solution)/shard_map/ppermute | solution.py:270
  498.1 27.7 %collective-permute-start.31 = (bf16[768,128]{1,0:T(8,128)(2,1)}, bf16[768,128]{1,0:T(8,128)(2,1)}, u32[]{:S(2)}, u32[]{:S(2)}) collective-permute-start(bf16[768,128]{1,0:T(8,128)(2,1)} %get-tuple-element.130), channel_id=1, source_target_pairs={{0,2},{1,3},{2,0},{3,1},{4,6},{5,7},{6,4},{7,5},{8,10},{9,11},{10,... | collective-permute-start | bytes 589832 | tf_op jit(solution)/shard_map/ppermute | solution.py:270
  498.8 27.9 %collective-permute-start.32 = (bf16[768,128]{1,0:T(8,128)(2,1)}, bf16[768,128]{1,0:T(8,128)(2,1)}, u32[]{:S(2)}, u32[]{:S(2)}) collective-permute-start(bf16[768,128]{1,0:T(8,128)(2,1)} %get-tuple-element.129), channel_id=1, source_target_pairs={{0,1},{1,2},{2,3},{3,0},{4,5},{5,6},{6,7},{7,4},{8,9},{9,10},{10,1... | collective-permute-start | bytes 589832 | tf_op jit(solution)/shard_map/ppermute | solution.py:270
  499.7 29.7 %collective-permute-start.18 = (bf16[768,128]{1,0:T(8,128)(2,1)}, bf16[768,128]{1,0:T(8,128)(2,1)}, u32[]{:S(2)}, u32[]{:S(2)}) collective-permute-start(bf16[768,128]{1,0:T(8,128)(2,1)} %get-tuple-element.143), channel_id=1, source_target_pairs={{0,3},{1,0},{2,1},{3,2},{4,7},{5,4},{6,5},{7,6},{8,11},{9,8},{10,9... | collective-permute-start | bytes 589832 | tf_op jit(solution)/shard_map/ppermute | solution.py:270
  503.5 39.1 %collective-permute-start.19 = (bf16[768,128]{1,0:T(8,128)(2,1)}, bf16[768,128]{1,0:T(8,128)(2,1)}, u32[]{:S(2)}, u32[]{:S(2)}) collective-permute-start(bf16[768,128]{1,0:T(8,128)(2,1)} %get-tuple-element.145), channel_id=1, source_target_pairs={{0,2},{1,3},{2,0},{3,1},{4,6},{5,7},{6,4},{7,5},{8,10},{9,11},{10,... | collective-permute-start | bytes 589832 | tf_op jit(solution)/shard_map/ppermute | solution.py:270
  508.9 7.1 %copy-start.31 = (bf16[1,256,128]{2,1,0:T(8,128)(2,1)S(1)}, bf16[1,256,128]{2,1,0:T(8,128)(2,1)}, u32[]{:S(2)}) copy-start(bf16[1,256,128]{2,1,0:T(8,128)(2,1)} %slice.422) | copy-start | bytes 196612
  509.6 34.0 %collective-permute-start.20 = (bf16[768,128]{1,0:T(8,128)(2,1)}, bf16[768,128]{1,0:T(8,128)(2,1)S(1)}, u32[]{:S(2)}, u32[]{:S(2)}) collective-permute-start(bf16[768,128]{1,0:T(8,128)(2,1)} %get-tuple-element.144), channel_id=1, source_target_pairs={{0,1},{1,2},{2,3},{3,0},{4,5},{5,6},{6,7},{7,4},{8,9},{9,10},{10,1... | collective-permute-start | bytes 589832 | tf_op jit(solution)/shard_map/ppermute | solution.py:270
  516.7 28.9 %copy-start.33 = (bf16[768,128]{1,0:T(8,128)(2,1)S(1)}, bf16[768,128]{1,0:T(8,128)(2,1)}, u32[]{:S(2)}) copy-start(bf16[768,128]{1,0:T(8,128)(2,1)} %copy-done.32) | copy-start | bytes 589828
  516.7 28.9 %copy-start.27 = (bf16[1,512,128]{2,1,0:T(8,128)(2,1)S(1)}, bf16[1,512,128]{2,1,0:T(8,128)(2,1)}, u32[]{:S(2)}) copy-start(bf16[1,512,128]{2,1,0:T(8,128)(2,1)} %slice.433) | copy-start | bytes 393220
  516.7 56.7 %reduce-scatter.14.cloned.1.call-start = ((), (), s32[]{:S(2)}) async-start(), calls=%async_computation.10 | async-start | bytes 737280 | tf_op jit(solution)/shard_map/reduce_scatter | solution.py:386
  525.8 26.5 %collective-permute-start.24 = (bf16[768,128]{1,0:T(8,128)(2,1)}, bf16[768,128]{1,0:T(8,128)(2,1)}, u32[]{:S(2)}, u32[]{:S(2)}) collective-permute-start(bf16[768,128]{1,0:T(8,128)(2,1)} %get-tuple-element.146), channel_id=1, source_target_pairs={{0,3},{1,0},{2,1},{3,2},{4,7},{5,4},{6,5},{7,6},{8,11},{9,8},{10,9... | collective-permute-start | bytes 589832 | tf_op jit(solution)/shard_map/ppermute | solution.py:270
  526.8 26.5 %collective-permute-start.25 = (bf16[768,128]{1,0:T(8,128)(2,1)}, bf16[768,128]{1,0:T(8,128)(2,1)}, u32[]{:S(2)}, u32[]{:S(2)}) collective-permute-start(bf16[768,128]{1,0:T(8,128)(2,1)} %get-tuple-element.148), channel_id=1, source_target_pairs={{0,2},{1,3},{2,0},{3,1},{4,6},{5,7},{6,4},{7,5},{8,10},{9,11},{10,... | collective-permute-start | bytes 589832 | tf_op jit(solution)/shard_map/ppermute | solution.py:270
  529.4 24.9 %collective-permute-start.26 = (bf16[768,128]{1,0:T(8,128)(2,1)}, bf16[768,128]{1,0:T(8,128)(2,1)}, u32[]{:S(2)}, u32[]{:S(2)}) collective-permute-start(bf16[768,128]{1,0:T(8,128)(2,1)} %get-tuple-element.147), channel_id=1, source_target_pairs={{0,1},{1,2},{2,3},{3,0},{4,5},{5,6},{6,7},{7,4},{8,9},{9,10},{10,1... | collective-permute-start | bytes 589832 | tf_op jit(solution)/shard_map/ppermute | solution.py:270
  550.6 46.9 %reduce-scatter.10.cloned.1.call-start = ((), (), s32[]{:S(2)}) async-start(), calls=%async_computation.8 | async-start | bytes 983040 | tf_op jit(solution)/shard_map/reduce_scatter | solution.py:394
  550.6 4.6 copy-start.34
  (27 other events, 45.6 us)
Sparse Core Ops, SparseCore 0:
  11.4 102.5 all-gather.3
  117.3 72.9 all-gather.5
  275.2 53.1 reduce-scatter.11
  332.1 60.1 reduce-scatter.7
  516.9 32.3 reduce-scatter.15
  551.4 21.9 reduce-scatter.13
  575.8 21.6 reduce-scatter.9

commit v2 on v1

v2 whole, which is shorter than its diff:
```python
import functools

import jax
import jax.numpy as jnp
from jax import lax
from jax.experimental import pallas as pl
from jax.experimental.pallas import tpu as pltpu
from jax.sharding import Mesh, PartitionSpec as P

HD = 64
CL = 128
PAIR = 2 * HD
WIDE = 4 * HD
F32 = jnp.float32
BF16 = jnp.bfloat16
EPS = 1e-06
PEAK_PER_MICRO = 1.15e9


def nn(left, right):
    return jnp.dot(left, right, preferred_element_type=F32)


def nt(left, right):
    return lax.dot_general(left, right, (((1,), (1,)), ((), ())), preferred_element_type=F32)


def tn(left, right):
    return lax.dot_general(left, right, (((0,), (0,)), ((), ())), preferred_element_type=F32)


def one_hot(hits):
    return jnp.where(hits, 1.0, 0.0).astype(BF16)


def head_lane(shape, dim, part):
    lane = lax.broadcasted_iota(jnp.int32, shape, dim)
    column = (lane // WIDE) * HD + lane % HD
    return jnp.where((lane % WIDE) // HD == part, column, -1)


def prepare_kernel(q_ref, k_ref, v_ref, o_ref, up_ref, dn_ref, heads_ref, ff_ref):
    shape = (q_ref.shape[1], heads_ref.shape[1])
    column = lax.broadcasted_iota(jnp.int32, shape, 0)
    total = jnp.zeros(heads_ref.shape, F32)
    for part, ref in ((0, q_ref), (1, v_ref), (2, k_ref)):
        total = total + nn(ref[...], one_hot(head_lane(shape, 1, part) == column))
    heads_ref[...] = total.astype(BF16)
    hidden = up_ref.shape[1]
    ff_ref[:, :hidden] = up_ref[...]
    ff_ref[:, hidden : 2 * hidden] = dn_ref[...]
    shape = (ff_ref.shape[1] - 2 * hidden, o_ref.shape[0])
    spread = one_hot(lax.broadcasted_iota(jnp.int32, shape, 0) == lax.broadcasted_iota(jnp.int32, shape, 1))
    padded = nn(spread, o_ref[...]).astype(BF16)
    rows = o_ref.shape[1]
    same = lax.broadcasted_iota(jnp.int32, (rows, rows), 0) == lax.broadcasted_iota(jnp.int32, (rows, rows), 1)
    ff_ref[:, 2 * hidden :] = nt(one_hot(same), padded).astype(BF16)


def unmix_kernel(grads_ref, q_ref, k_ref, v_ref):
    shape = (q_ref.shape[1], grads_ref.shape[1])
    column = lax.broadcasted_iota(jnp.int32, shape, 0)
    for part, ref in ((0, q_ref), (1, v_ref), (2, k_ref)):
        ref[...] = nt(grads_ref[...], one_hot(head_lane(shape, 1, part) == column))


def order_kernel(seqs, scal_ref, clusters_ref, balance_ref, order_ref, seg_ref):
    count = balance_ref.shape[1]
    step = 2 * CL
    rows = scal_ref[2]
    balance = balance_ref[...]
    high = balance // HD
    low = balance - high * HD
    pick = lax.broadcasted_iota(jnp.int32, (8, count), 0)
    table = jnp.where(pick == 0, high, jnp.where(pick == 1, low, 0)).astype(F32).astype(BF16)
    chosen = clusters_ref[0]
    total = jnp.zeros((8, count), F32)
    for start in range(0, count, step):
        place = lax.broadcasted_iota(jnp.int32, (step, count), 0) + start
        total = total + nn(table[:, start : start + step], one_hot(place == chosen))
    token = (total[0:1] * float(HD) + total[1:2]).astype(jnp.int32)
    segment = jnp.zeros_like(token)
    for s in range(seqs):
        segment = segment + jnp.where(token >= scal_ref[3 + s], 1, 0)
    seg_ref[0] = segment.astype(F32)
    from_own = scal_ref[0] * rows - (token // rows) * rows
    from_own = jnp.where(from_own < 0, from_own + count, from_own)
    order_ref[0] = (from_own + token % rows).astype(F32)


def column_of(row):
    return jnp.transpose(jnp.broadcast_to(row, (CL, CL)))


def slots_by_tokens(order_ref, start, span, count):
    lane = lax.broadcasted_iota(jnp.int32, (CL, CL), 1).astype(F32)
    parts = []
    for at in range(0, span, CL):
        gap = column_of(order_ref[0, :, pl.ds(start + at, CL)]) - lane
        parts.append(jnp.concatenate([one_hot(gap == float(j)) for j in range(0, count, CL)], axis=1))
    return jnp.concatenate(parts, axis=0)


def tokens_by_slots(order_ref, start, span, count):
    row = order_ref[0] - jnp.asarray(start, F32)
    return one_hot(lax.broadcasted_iota(jnp.int32, (span, count), 0).astype(F32) == row)


def softmax_of(first, second, seg_ref, start):
    scores = nt(first, second) * HD ** (-0.5)
    seg_row = seg_ref[0, :, pl.ds(start, CL)]
    scores = jnp.where(column_of(seg_row) == seg_row, scores, -1e30)
    raised = jnp.exp(scores - jnp.max(scores, axis=1, keepdims=True))
    return raised / jnp.sum(raised, axis=1, keepdims=True)


def upper_half(values):
    lane = lax.broadcasted_iota(jnp.int32, values.shape, 1)
    return jnp.where(lane >= HD, values, 0.0)


def project_kernel(size, heads, scal_ref, own_ref, w_ref, b_ref, *refs):
    ups, downs = refs[: size - 1], refs[size - 1 : 2 * size - 2]
    x_out, qkv_out, x_ref, qkv_ref, in_sem, x_sem, qkv_sem = refs[2 * size - 2 :]
    rows = own_ref.shape[0]
    rank = scal_ref[0]

    def place(k):
        return pl.ds(k * rows, rows)

    def landing(k, source):
        return pltpu.make_async_copy(source, x_ref.at[place(k)], in_sem.at[k])

    landing(0, own_ref).start()
    for k in range(1, size):

        @pl.when(rank >= k)
        def _(k=k):
            landing(k, ups[k - 1]).start()

        @pl.when(rank < k)
        def _(k=k):
            landing(k, downs[size - 1 - k]).start()

    leaving = []
    for k in range(size):
        landing(k, own_ref).wait()
        leaving.append(pltpu.make_async_copy(x_ref.at[place(k)], x_out.at[place(k)], x_sem.at[k]))
        leaving[-1].start()
        for h in range(heads):
            lanes = slice(h * WIDE, (h + 1) * WIDE)
            qkv_ref[h, place(k)] = (nn(x_ref[place(k)], w_ref[:, lanes]) + b_ref[:, lanes]).astype(BF16)
            leaving.append(
                pltpu.make_async_copy(qkv_ref.at[h, place(k)], qkv_out.at[h, place(k)], qkv_sem.at[h, k])
            )
            leaving[-1].start()
    for copy in leaving:
        copy.wait()


def forward_kernel(size, heads, span, scal_ref, order_ref, seg_ref, qkv_ref, extra_ref, slots_ref, out_ref, ctx_ref):
    head = pl.program_id(0)
    count = qkv_ref.shape[1]
    rows = count // size
    half = rows // 2
    for k in range(size):
        out_ref[k, pl.ds(heads * half, extra_ref.shape[0])] = extra_ref[...]

    def gather(i, carry):
        start = pl.multiple_of(i * span, span)
        picked = nn(slots_by_tokens(order_ref, start, span, count), qkv_ref[0]).astype(BF16)
        slots_ref[0, pl.ds(start, span)] = picked
        for at in range(0, span, CL):
            first, second = picked[at : at + CL, :PAIR], picked[at : at + CL, PAIR:]
            probs = softmax_of(first, second, seg_ref, start + at)
            ctx_ref[pl.ds(start + at, CL)] = upper_half(nn(probs.astype(BF16), first)).astype(BF16)
        return carry

    lax.fori_loop(0, count // span, gather, 0)
    at = pl.ds(pl.multiple_of(head * half, half), half)
    for k in range(size):
        given = nn(tokens_by_slots(order_ref, k * rows, rows, count), ctx_ref[...])
        to = lax.rem(scal_ref[0] - k + size, size)
        out_ref[to, at] = (pltpu.roll(given[:half], HD, 1) + given[half:]).astype(BF16)


def backward_kernel(size, span, order_ref, seg_ref, slots_ref, turned_ref, *refs):
    g_refs, outs = refs[:size], refs[size : 2 * size]
    mine_ref, other_ref, bias_ref, gctx_ref, grad_ref, tok_ref = refs[2 * size :]
    count = slots_ref.shape[1]
    rows = count // size
    half = rows // 2
    for k in range(size):
        packed = g_refs[k][...].astype(F32)
        gctx_ref[k * rows : k * rows + half] = upper_half(pltpu.roll(packed, HD, 1)).astype(BF16)
        gctx_ref[k * rows + half : (k + 1) * rows] = upper_half(packed).astype(BF16)

    def gather(i, sums):
        start = pl.multiple_of(i * span, span)
        picked = nn(slots_by_tokens(order_ref, start, span, count), gctx_ref[...]).astype(BF16)
        lane = lax.broadcasted_iota(jnp.int32, (CL, PAIR), 1)
        for offset in range(0, span, CL):
            at = pl.ds(start + offset, CL)
            part = slots_ref[0, at]
            first, second = part[:, :PAIR], part[:, PAIR:]
            grad_ctx = picked[offset : offset + CL]
            probs = softmax_of(first, second, seg_ref, start + offset)
            grad_prob = nt(grad_ctx, first)
            inner = jnp.sum(probs * grad_prob, axis=1, keepdims=True)
            grad_scores = (probs * (grad_prob - inner)).astype(BF16)
            grad_query = nn(grad_scores, second) * HD ** (-0.5)
            grad_key = tn(grad_scores, first) * HD ** (-0.5)
            grad_value = tn(probs.astype(BF16), grad_ctx)
            grad_qv = jnp.where(lane < HD, grad_query, grad_value).astype(BF16)
            sums = sums + jnp.sum(grad_qv.astype(F32), axis=0, keepdims=True)
            grad_ref[at, :PAIR] = grad_qv
            grad_ref[at, PAIR:] = jnp.where(lane < HD, grad_key, 0.0).astype(BF16)
        return sums

    bias_ref[...] = lax.fori_loop(0, count // span, gather, jnp.zeros((1, PAIR), F32))
    for k in range(size):
        given = nn(tokens_by_slots(order_ref, k * rows, rows, count), grad_ref[...])
        low = given.astype(BF16)
        tok_ref[k * rows : (k + 1) * rows] = low
        outs[k][:rows] = low[:, :PAIR]
        outs[k][rows:] = (given[:half, PAIR:] + pltpu.roll(given[half:, PAIR:], HD, 1)).astype(BF16)
    cut = turned_ref.shape[0] // 2
    mine_ref[...] = nn(turned_ref[:cut], tok_ref[...]).astype(BF16)
    other_ref[...] = nn(turned_ref[cut:], tok_ref[...]).astype(BF16)


def row_stats(values_in):
    center = values_in - jnp.mean(values_in, axis=-1, keepdims=True)
    inverse = lax.rsqrt(jnp.mean(center * center, axis=-1, keepdims=True) + EPS)
    return center * inverse, inverse


def norm_back(cotangent, gain, hat, inverse):
    scaled = cotangent * gain
    return inverse * (
        scaled
        - jnp.mean(scaled, axis=-1, keepdims=True)
        - hat * jnp.mean(scaled * hat, axis=-1, keepdims=True)
    )


def column_sum(values_in):
    return jnp.sum(values_in, axis=0, keepdims=True)


def row_copies(ref, layout, start, lanes, held, sem):
    size, groups, shard = layout
    if groups == 1:
        shard = held.shape[0]
    return [
        pltpu.make_async_copy(
            ref.at[pl.ds((group * size + k) * shard, shard), pl.ds(start, lanes)],
            held.at[pl.ds(group * shard, shard), pl.ds(k * lanes, lanes)],
            sem,
        )
        for group in range(groups)
        for k in range(size)
    ]


def all_of(held, sem):
    return pltpu.make_async_copy(held, held, sem)


def layer_kernel(heads, layout, scal_ref, x_ref, og_ref, vec_ref, recv_ref, *refs):
    size = layout[0]
    ff_ref, refs = refs[0], refs[1:]
    layer_ref, sum_ref, act_out, gup_out, nlow_ref, plow_ref, slow_ref, ctx_ref, small_ref = refs[:9]
    gctx_refs = refs[9 : 9 + size]
    wup_ref, wdn_ref, wo_ref, act_ref, gup_ref, slope_ref, total_ref = refs[9 + size : 16 + size]
    sem, out_sem = refs[16 + size :]
    rows, width = x_ref.shape
    hidden = wup_ref.shape[1] // size
    head_lanes = wo_ref.shape[1] // size
    rank = scal_ref[0]

    for kind, (start, lanes, held) in enumerate(
        ((2 * hidden, head_lanes, wo_ref), (0, hidden, wup_ref), (hidden, hidden, wdn_ref))
    ):
        for copy in row_copies(ff_ref, layout, start, lanes, held, sem.at[kind]):
            copy.start()

    half = rows // 2
    lower = lax.broadcasted_iota(jnp.int32, (half, PAIR), 1) < HD
    source = [lax.rem(rank - k + size, size) for k in range(size)]
    for k in range(size):
        for h in range(0, heads, 2):
            first = recv_ref[source[k], h * half : (h + 1) * half].astype(F32)
            second = jnp.zeros((half, PAIR), F32)
            if h + 1 < heads:
                second = recv_ref[source[k], (h + 1) * half : (h + 2) * half].astype(F32)
            lanes = slice(k * head_lanes + h * HD, k * head_lanes + h * HD + PAIR)
            ctx_ref[:half, lanes] = jnp.where(lower, first, pltpu.roll(second, HD, 1)).astype(BF16)
            ctx_ref[half:, lanes] = jnp.where(lower, pltpu.roll(first, HD, 1), second).astype(BF16)
    all_of(wo_ref, sem.at[0]).wait()
    summed = x_ref[...].astype(F32) + nt(ctx_ref[...], wo_ref[...]) + vec_ref[0:1]
    hat1, inverse1 = row_stats(summed)
    normed = hat1 * vec_ref[1:2] + vec_ref[2:3]
    nlow_ref[...] = normed.astype(BF16)
    all_of(wup_ref, sem.at[1]).wait()

    total_ref[...] = normed + vec_ref[3:4]
    curve = (2.0 / 3.141592653589793) ** 0.5
    cut = hidden // PAIR
    all_of(wdn_ref, sem.at[2]).wait()

    def leave(kept, out, kind, lanes):
        return pltpu.make_async_copy(kept.at[:, lanes], out.at[:, lanes], out_sem.at[kind])

    def span(k):
        return pl.ds(pl.multiple_of(k * hidden, hidden), hidden)

    def forward(k, carry):
        lanes = span(k)
        parts = recv_ref[lax.rem(rank - k + size, size), heads * half :].astype(F32)
        bias = parts[:cut] + parts[cut : 2 * cut] + parts[2 * cut : 3 * cut]
        bias = jnp.concatenate([bias[i : i + 1] for i in range(cut)], axis=1)
        up = nn(nlow_ref[...], wup_ref[:, lanes]) + bias
        square = up * up
        tanh = jnp.tanh(up * (curve + (0.044715 * curve) * square))
        gate = 0.5 + 0.5 * tanh
        act_ref[:, lanes] = (up * gate).astype(BF16)
        slope_ref[:, lanes] = gate + (0.5 * up) * (1.0 - tanh * tanh) * (curve + (3 * 0.044715 * curve) * square)
        leave(act_ref, act_out, 0, lanes).start()
        total_ref[...] += nt(act_ref[:, lanes], wdn_ref[:, lanes])
        return carry

    lax.fori_loop(0, size, forward, 0)
    hat2, inverse2 = row_stats(total_ref[...])
    gain2 = vec_ref[4:5]
    layer_ref[...] = (hat2 * gain2 + vec_ref[5:6]).astype(BF16)
    cot = og_ref[...].astype(F32)
    grad_pre = norm_back(cot, gain2, hat2, inverse2)
    plow_ref[...] = grad_pre.astype(BF16)
    small_ref[3:4] = column_sum(grad_pre)
    small_ref[4:5] = column_sum(cot * hat2)
    small_ref[5:6] = column_sum(cot)
    small_ref[6:8] = jnp.zeros((2, width), F32)
    total_ref[...] = grad_pre

    def backward(k, carry):
        lanes = span(k)
        grad_up = (nn(plow_ref[...], wdn_ref[:, lanes]) * slope_ref[:, lanes]).astype(BF16)
        gup_ref[:, lanes] = grad_up
        leave(gup_ref, gup_out, 1, lanes).start()
        small_ref[pl.ds(8 + lax.rem(rank - k + size, size), 1)] = column_sum(grad_up.astype(F32))
        total_ref[...] += nt(gup_ref[:, lanes], wup_ref[:, lanes])
        return carry

    lax.fori_loop(0, size, backward, 0)
    grad_normed = total_ref[...]
    small_ref[1:2] = column_sum(grad_normed * hat1)
    small_ref[2:3] = column_sum(grad_normed)
    grad_summed = norm_back(grad_normed, vec_ref[1:2], hat1, inverse1)
    small_ref[0:1] = column_sum(grad_summed)
    sum_ref[...] = grad_summed
    slow_ref[...] = grad_summed.astype(BF16)
    grad_ctx = nn(slow_ref[...], wo_ref[...])
    for k in range(size):
        for h in range(0, heads, 2):
            lanes = slice(k * head_lanes + h * HD, k * head_lanes + h * HD + PAIR)
            top, bottom = grad_ctx[:half, lanes], grad_ctx[half:, lanes]
            gctx_refs[k][h * half : (h + 1) * half] = jnp.where(lower, top, pltpu.roll(bottom, HD, 1)).astype(BF16)
            if h + 1 < heads:
                gctx_refs[k][(h + 1) * half : (h + 2) * half] = jnp.where(
                    lower, pltpu.roll(top, HD, 1), bottom
                ).astype(BF16)
    pltpu.make_async_copy(act_ref, act_out, out_sem.at[0]).wait()
    pltpu.make_async_copy(gup_ref, gup_out, out_sem.at[1]).wait()


def turned_kernel(pairs, *refs):
    lefts, rights = refs[:pairs], refs[pairs : 2 * pairs]
    out_ref, turned_ref = refs[2 * pairs :]
    width = out_ref.shape[0]

    @pl.when(pl.program_id(0) == 0)
    def _():
        row = lax.broadcasted_iota(jnp.int32, (width, width), 0)
        same = one_hot(row == lax.broadcasted_iota(jnp.int32, (width, width), 1))
        for i in range(pairs):
            turned_ref[i] = nt(same, lefts[i][...]).astype(BF16)

    at = 0
    for i in range(pairs):
        lanes = slice(at, at + rights[i].shape[1])
        at = lanes.stop
        out_ref[:, lanes] = nn(turned_ref[i], rights[i][...]).astype(BF16)


def flip_kernel(pick_ref, left_ref, turned_ref):
    turned_ref[...] = nt(pick_ref[...], left_ref[...]).astype(BF16)


def finish_kernel(head, layout, acc_ref, w_ref, *refs):
    size = layout[0]
    out_ref, held_ref, grads_ref, sem = refs[-4:]
    g_refs = refs[:size]
    rows = acc_ref.shape[0]
    half = rows // 2
    for copy in row_copies(w_ref, layout, head * WIDE, WIDE, held_ref, sem):
        copy.start()
    lower = lax.broadcasted_iota(jnp.int32, (half, PAIR), 1) < HD
    for k in range(size):
        at = k * WIDE
        grads_ref[:, at : at + PAIR] = g_refs[k][:rows]
        packed = g_refs[k][rows:].astype(F32)
        grads_ref[:half, at + PAIR : at + WIDE] = jnp.where(lower, packed, 0.0).astype(BF16)
        grads_ref[half:, at + PAIR : at + WIDE] = jnp.where(lower, pltpu.roll(packed, HD, 1), 0.0).astype(BF16)
    all_of(held_ref, sem).wait()
    out_ref[...] = acc_ref[...] + nt(grads_ref[...], held_ref[...])


def cost(micros, exps=0):
    return pl.CostEstimate(flops=int(micros * PEAK_PER_MICRO), bytes_accessed=0, transcendentals=int(exps))


def head_spec(shape, head):
    return pl.BlockSpec((1,) + shape, lambda i: (head,) + (0,) * len(shape))


def full(shape):
    return pl.BlockSpec(tuple(shape), lambda i: (0,) * len(shape))


def held():
    return pl.BlockSpec(memory_space=pl.ANY)


def scalars_spec():
    return pl.BlockSpec(memory_space=pltpu.SMEM)


def shape_of(shape, dtype=BF16):
    return jax.ShapeDtypeStruct(tuple(shape), dtype)


def call(kernel, name, in_specs, out_specs, out_shape, scratch, estimate, mib, grid=(1,), after=()):
    count = len(in_specs)

    def body(*refs):
        kernel(*refs[:count], *refs[count + len(after) :])

    run = pl.pallas_call(
        body,
        grid=grid,
        in_specs=list(in_specs) + [held()] * len(after),
        out_specs=out_specs,
        out_shape=out_shape,
        scratch_shapes=scratch,
        compiler_params=pltpu.CompilerParams(vmem_limit_bytes=mib * 1024 * 1024),
        name=name,
        cost_estimate=estimate,
    )
    return lambda *args: run(*args, *after)


def prepare(query, key, value, out, up, down_t, heads):
    shard, hidden = up.shape
    lanes = 2 * hidden + -(-out.shape[0] // CL) * CL
    args = (query, key, value, out, up, down_t)
    shapes = [shape_of((shard, heads * WIDE)), shape_of((shard, lanes))]
    return call(
        prepare_kernel, "prepare", [full(a.shape) for a in args], [full(s.shape) for s in shapes], shapes, [],
        cost(1), 16,
    )(*args)


def unmix(grads, local_width):
    shard = grads.shape[0]
    shapes = [shape_of((shard, local_width), F32)] * 3
    return call(
        unmix_kernel, "unmix", [full(grads.shape)], [full(s.shape) for s in shapes], shapes, [],
        cost(1), 16,
    )(grads)


def slot_tokens(seqs, scalars, clusters, balance):
    heads, count = clusters.shape[0], clusters.shape[2]
    row = pl.BlockSpec((1, 1, count), lambda h: (h, 0, 0))
    return call(
        functools.partial(order_kernel, seqs), "slot_tokens",
        [scalars_spec(), row, full(balance.shape)], [row] * 2, [shape_of((heads, 1, count), F32)] * 2, [],
        cost(8), 16, grid=(heads,),
    )(scalars, clusters, balance)


def project(size, heads, scalars, own, weights, biases, ups, downs, after):
    rows, width = own.shape
    lanes = heads * WIDE
    shapes = [shape_of((size * rows, width)), shape_of((heads, size * rows, WIDE))]
    return call(
        functools.partial(project_kernel, size, heads), "project",
        [scalars_spec(), held(), full(weights.shape), full(biases.shape)] + [held()] * (2 * size - 2),
        [held()] * 2, shapes,
        [pltpu.VMEM(s.shape, BF16) for s in shapes]
        + [pltpu.SemaphoreType.DMA((size,)), pltpu.SemaphoreType.DMA((size,)), pltpu.SemaphoreType.DMA((heads, size))],
        cost(6), 24, after=after,
    )(scalars, own, weights, biases, *ups, *downs)


def attend(size, scalars, order, seg, qkv, extra):
    heads, count = qkv.shape[:2]
    half = count // size // 2
    row = pl.BlockSpec((1, 1, count), lambda h: (h, 0, 0))
    block = pl.BlockSpec((1, count, WIDE), lambda h: (h, 0, 0))
    shapes = [shape_of((heads, count, WIDE)), shape_of((size, heads * half + extra.shape[0], PAIR))]
    return call(
        functools.partial(forward_kernel, size, heads, count // 2), "attend",
        [scalars_spec(), row, row, block, full(extra.shape)],
        [block, full(shapes[1].shape)], shapes,
        [pltpu.VMEM((count, PAIR), BF16)],
        cost(30), 32, grid=(heads,),
    )(scalars, order, seg, qkv, extra)


def attend_back(size, head, order, seg, slots, turned_x, grad_context, after):
    count = slots.shape[1]
    rows = count // size
    cut = turned_x.shape[0] // 2
    shapes = (
        [shape_of((rows + rows // 2, PAIR))] * size + [shape_of((cut, WIDE))] * 2 + [shape_of((1, PAIR), F32)]
    )
    return call(
        functools.partial(backward_kernel, size, count // 2), "attend_back",
        [head_spec((1, count), head), head_spec((1, count), head), head_spec((count, WIDE), head), full(turned_x.shape)]
        + [pl.BlockSpec((rows // 2, PAIR), lambda i: (head, 0))] * size,
        [full(s.shape) for s in shapes], shapes,
        [pltpu.VMEM((count, PAIR), BF16), pltpu.VMEM((count, WIDE), BF16), pltpu.VMEM((count, WIDE), BF16)],
        cost(3), 40, after=after,
    )(order, seg, slots, turned_x, *grad_context)


def layer(heads, layout, hidden, scalars, inputs, out_grad, vectors, received, ff, after):
    size = layout[0]
    rows, width = inputs.shape
    head_lanes = ff.shape[1] - 2 * hidden
    shapes = [
        shape_of((rows, width)),
        shape_of((rows, width), F32),
        shape_of((rows, size * hidden)),
        shape_of((rows, size * hidden)),
        shape_of((rows, width)),
        shape_of((rows, width)),
        shape_of((rows, width)),
        shape_of((rows, size * head_lanes)),
        shape_of((8 + size, width), F32),
    ] + [shape_of((heads * (rows // 2), PAIR))] * size
    args = (inputs, out_grad, vectors, received)
    return call(
        functools.partial(layer_kernel, heads, layout), "layer",
        [scalars_spec()] + [full(a.shape) for a in args] + [held()],
        [full(s.shape) if i not in (2, 3) else held() for i, s in enumerate(shapes)], shapes,
        [
            pltpu.VMEM((width, size * hidden), BF16),
            pltpu.VMEM((width, size * hidden), BF16),
            pltpu.VMEM((width, size * head_lanes), BF16),
            pltpu.VMEM((rows, size * hidden), BF16),
            pltpu.VMEM((rows, size * hidden), BF16),
            pltpu.VMEM((rows, size * hidden), F32),
            pltpu.VMEM((rows, width), F32),
            pltpu.SemaphoreType.DMA((3,)),
            pltpu.SemaphoreType.DMA((2,)),
        ],
        cost(24), 56, after=after,
    )(scalars, *args, ff)


def turned(size, lefts, rights):
    rows, width = lefts[0].shape
    columns = sum(right.shape[1] for right in rights)
    return call(
        functools.partial(turned_kernel, len(lefts)), "turned",
        [full(left.shape) for left in lefts]
        + [pl.BlockSpec((rows, right.shape[1] // size), lambda i: (0, i)) for right in rights],
        pl.BlockSpec((width, columns // size), lambda i: (0, i)), shape_of((width, columns)),
        [pltpu.VMEM((len(lefts), width, rows), BF16)],
        cost(1), 32, grid=(size,),
    )(*lefts, *rights)


def flip(size, pick, left):
    count, width = left.shape
    rows = count // size
    return call(
        flip_kernel, "flip",
        [full(pick.shape), pl.BlockSpec((rows, width), lambda i: (i, 0))],
        pl.BlockSpec((width, rows), lambda i: (0, i)), shape_of((width, count)), [],
        cost(1), 16, grid=(size,),
    )(pick, left)


def finish(head, layout, total, weights, grads, after):
    size = layout[0]
    rows, width = total.shape
    return call(
        functools.partial(finish_kernel, head, layout), "finish",
        [full(total.shape), held()] + [full(g.shape) for g in grads],
        full(total.shape), shape_of(total.shape, F32),
        [
            pltpu.VMEM((width, size * WIDE), BF16),
            pltpu.VMEM((rows, size * WIDE), BF16),
            pltpu.SemaphoreType.DMA(()),
        ],
        cost(1), 24, after=after,
    )(total, weights, *grads)


def shift(values, size, k):
    return lax.ppermute(values, "tensor", [(i, (i + k) % size) for i in range(size)])


def exchange(parts, size):
    return [parts[0]] + [shift(parts[size - k], size, k) for k in range(1, size)]


def gather_line(own, size):
    up, down = own, own
    ups, downs = [], []
    for k in range(1, size):
        up = lax.ppermute(up, "tensor", [(i, i + 1) for i in range(k - 1, size - 1)])
        down = lax.ppermute(down, "tensor", [(i + 1, i) for i in range(0, size - k)])
        ups.append(up)
        downs.append(down)
    return ups, downs


def swap(values, axis, bit):
    return lax.ppermute(values, axis, [(i, i ^ bit) for i in range(lax.axis_size(axis))])


def bits_of(size):
    return [1 << b for b in range(size.bit_length() - 1)]


def add_low(left, right):
    return (left.astype(F32) + right.astype(F32)).astype(BF16)


def halves(mine, arrived):
    cut = mine.shape[0] // 2
    return add_low(mine[:cut], arrived[:cut]), add_low(mine[cut:], arrived[cut:])


def total_of(parts):
    result = parts[0].astype(F32)
    for part in parts[1:]:
        result = result + part.astype(F32)
    return result


def tie(*groups):
    return lax.optimization_barrier(groups)


def local(
    inputs, out_grad, seq_lengths, balance, clusters, query_weight, query_bias, key_weight,
    value_weight, value_bias, out_weight, out_bias, norm1_gain, norm1_bias, up_weight, up_bias,
    down_weight, down_bias, norm2_gain, norm2_bias,
):
    dp = ("chip", "core")
    rows, width = inputs.shape
    size = lax.axis_size("tensor")
    chips = lax.axis_size("chip")
    rank, chip, core = (lax.axis_index(axis) for axis in ("tensor", "chip", "core"))
    shard = query_weight.shape[0]
    local_width = query_weight.shape[1]
    heads = clusters.shape[1]
    seqs = seq_lengths.shape[1]
    bits = bits_of(chips)

    bounds = jnp.cumsum(seq_lengths[0])
    scalars = jnp.concatenate([jnp.stack([rank, core, jnp.int32(rows)]), bounds]).astype(jnp.int32)
    direct = shard % 16 == 0
    layout = (size, 2 * chips if direct else 1, shard)
    hidden = up_weight.shape[1]

    def near_of(own):
        ups, downs = gather_line(own, size)
        return jnp.concatenate(
            [own] + [jnp.where(rank >= k, ups[k - 1], downs[size - 1 - k]) for k in range(1, size)], axis=0
        )

    def whole(near):
        rows_in = lax.all_gather(near, dp, axis=0, tiled=True)
        if direct:
            return rows_in
        lanes = near.shape[1]
        return rows_in.reshape(2 * chips, size, shard, lanes).transpose(1, 0, 2, 3).reshape(size * width, lanes)

    head_weights, ff_own = prepare(
        query_weight, key_weight, value_weight, out_weight, up_weight, down_weight.T, heads
    )
    ups, downs = gather_line(inputs, size)
    own_qkv = lax.all_gather(head_weights, dp, axis=0, tiled=True)
    near, own_qkv, ups[0], downs[0] = tie(near_of(ff_own), own_qkv, ups[0], downs[0])
    ff = whole(near)
    blank = jnp.zeros((heads, HD), F32)
    head_biases = jnp.concatenate(
        [query_bias.reshape(heads, HD), value_bias.reshape(heads, HD), blank, blank], axis=-1
    ).reshape(1, heads * WIDE)
    terms, rest = [], up_bias
    for _ in range(3):
        term = lax.reduce_precision(rest, 8, 7)
        terms.append(term.astype(BF16))
        rest = rest - term
    extra = jnp.concatenate(terms).reshape(-1, PAIR)
    extra = jnp.pad(extra, ((0, -extra.shape[0] % 16), (0, 0)))
    vectors = jnp.stack([out_bias, norm1_gain, norm1_bias, down_bias, norm2_gain, norm2_bias])

    def row_pick(order_bits):
        place = jnp.arange(width, dtype=jnp.int32)
        block = place // shard
        away = jnp.zeros_like(block)
        for depth, bit in enumerate(order_bits):
            away = away + ((block >> (len(order_bits) - 1 - depth)) & 1) * bit
        near = chip ^ away
        owner = near * 2 + (core ^ (block // chips))
        return one_hot((owner * shard + place % shard)[:, None] == place[None, :])

    pick = row_pick(bits)
    order, seg = slot_tokens(seqs, scalars, clusters[0][:, None, :], balance)
    x_all, qkv = project(size, heads, scalars, inputs, own_qkv, head_biases, ups, downs, [order])
    later_weights, qkv = tie(head_weights, qkv)
    later = whole(jnp.concatenate([later_weights] + [shift(later_weights, size, k) for k in range(1, size)], axis=0))

    slots, sent = attend(size, scalars, order, seg, qkv, extra)
    received = lax.all_to_all(sent, "tensor", 0, 0, tiled=True)
    turned_x = flip(size, pick, x_all)
    (layer_out, grad_summed, active, grad_up, normed_low, pre_low, summed_low, context, small, *grad_ctx) = layer(
        heads, layout, hidden, scalars, inputs, out_grad, vectors, received, ff, []
    )
    arrived = exchange(grad_ctx, size)

    grads = turned(size, [normed_low, pre_low, summed_low], [grad_up, active, context])
    first = [grads]
    grads = lax.psum_scatter(grads, dp, scatter_dimension=0, tiled=True)

    backs, head_mine, head_other, bias_sums = [], [], [], []
    for h in range(heads):
        after = backs[h - 2][1:] if h >= 2 else first
        outs = attend_back(size, h, order, seg, slots, turned_x, arrived, after)
        backs.append(exchange(outs[:size], size))
        head_mine.append(outs[size])
        head_other.append(outs[size + 1])
        bias_sums.append(outs[size + 2])
        if h < len(bits_of(size)):
            small = small + swap(small, "tensor", bits_of(size)[h])
            arrived, small = tie(arrived, small)
    mine = jnp.concatenate(head_mine, axis=1)
    far = swap(jnp.concatenate(head_other, axis=1), "core", 1)
    sums = jnp.concatenate([small, jnp.pad(jnp.concatenate(bias_sums, axis=0), ((0, 0), (0, width - PAIR)))], axis=0)
    sums = sums + swap(sums, "core", 1)
    for bit in bits:
        mine, sent = halves(mine, far)
        far = swap(sent, "chip", bit)
        sums = sums + swap(sums, "chip", bit)
    head_sum = add_low(mine, far)
    grad_inputs = grad_summed
    for h in range(heads):
        grad_inputs = finish(h, layout, grad_inputs, later, backs[h], [grads])
    grad_query_weight, grad_key_weight, grad_value_weight = unmix(head_sum, local_width)
    bias = sums[small.shape[0] :]
    grad_query_bias = bias[:, :HD].reshape(local_width)
    grad_value_bias = bias[:, HD:PAIR].reshape(local_width)
    grad_up_bias = lax.dynamic_index_in_dim(sums, 8 + rank, 0, keepdims=False)
    lanes = grads.shape[1] // size
    grads = total_of(exchange([grads[:, k * lanes : (k + 1) * lanes] for k in range(size)], size))
    grad_up_weight = grads[:, :hidden]
    grad_down_weight = grads[:, hidden : 2 * hidden].T
    grad_out_weight = grads[:, 2 * hidden : 2 * hidden + local_width].T
    return (
        layer_out, grad_inputs, grad_query_weight, grad_query_bias, grad_key_weight, grad_value_weight,
        grad_value_bias, grad_out_weight, sums[0], sums[1], sums[2], grad_up_weight, grad_up_bias,
        grad_down_weight, sums[3], sums[4], sums[5],
    )


def solution(mesh):
    devices = mesh.devices
    split = Mesh(devices.reshape(devices.shape[0] // 2, 2, devices.shape[1]), ("chip", "core", "tensor"))
    dp = ("chip", "core")
    rows, weight, turned_weight, vector, same = (
        P(dp + ("tensor",), None),
        P(dp, "tensor"),
        P("tensor", dp),
        P("tensor"),
        P(),
    )
    in_specs = (
        rows, rows, P(dp, None), P(dp, None), P(dp, "tensor", None), weight, vector, weight, weight,
        vector, turned_weight, same, same, same, weight, vector, turned_weight, same, same, same,
    )
    out_specs = (
        rows, rows, weight, vector, weight, weight, vector, turned_weight, same, same, same, weight, vector,
        turned_weight, same, same, same,
    )
    return jax.shard_map(local, mesh=split, in_specs=in_specs, out_specs=out_specs, check_vma=False)
```

time: 618 us -> 396 us (0.64)
  blocking collectives: 134 us -> 0 us
  local copies, waits for them, and re-layouts: 127 us -> 35.5 us
  Pallas kernels: 92.6 us -> 139 us
  matrix products: 45.4 us -> 0 us
  other arithmetic: 46.5 us -> 7.09 us
  waiting for transfers between devices: 88.3 us -> 120 us
  starting transfers between devices: 58.8 us -> 73.4 us
    all_gather x2 -> x0, blocking collectives: 82.4 us -> none  [the longest x1 66.5 us: local(): up_bias_full = lax.all_gather(up_bias, 'tensor', axis=0, tiled=True)]
    psum x2 -> x0, blocking collectives: 51.3 us -> none  [the longest x1 39.5 us: local(): lax.psum(jnp.concatenate([jnp.sum(grad_summed, axis=0), jnp.sum(grad_norm...]
    pallas_call x7 -> x14, Pallas kernels: 92.6 us -> 139 us  [call(): return lambda *args: run(*args, *after)]
    dot_general x15 -> x0, matrix products: 45.4 us -> none  [the longest x6 16.7 us: nt(): lax.dot_general(left, right, (((1,), (1,)), ((), ())), preferred_element_...]
    reshape x15 -> x1, local copies, waits for them, and re-layouts: 35.7 us -> 0.64 us  [local(): grad_value_bias = bias[:, HD:PAIR].reshape(local_width)]
    ppermute x27 -> x26, waiting for transfers between devices: 18.9 us -> 52 us  [the longest x18 36.5 us: shift(): lax.ppermute(values, 'tensor', [(i, (i + k) % size) for i in range(size)])]
    ppermute x3 -> x6, waiting for transfers between devices: 21.8 us -> 51.6 us  [gather_line(): lax.ppermute(down, 'tensor', [(i + 1, i) for i in range(0, size - k)])]
    reduce_scatter x4 -> x1, waiting for transfers between devices: 24.4 us -> 0.01 us  [local(): grads = lax.psum_scatter(grads, dp, scatter_dimension=0, tiled=True)]
  transfers between devices with their start and end apart: 40 -> 43, of which waited for: 12 -> 13; matrix products, arithmetic and copies ran while one was open for 34% -> 3% of each run, Pallas kernels for 15% -> 26%
where the time goes in v2:
time: 396 us; the launch traced here: 389 us
  Pallas kernels  139 us (35%)
  waiting for transfers between devices  120 us (30%)
  starting transfers between devices  73.4 us (19%)
  local copies, waits for them, and re-layouts  35.5 us (9%)
  between operations  14.9 us (4%)
  other arithmetic  7.09 us (2%)
    pallas_call x14, Pallas kernels, call(): return lambda *args: run(*args, *after)  139 us
    ppermute x6, waiting for transfers between devices, gather_line(): lax.ppermute(down, 'tensor', [(i + 1, i) for i in range(0, size - k)])  51.6 us
    ppermute x18, waiting for transfers between devices, shift(): lax.ppermute(values, 'tensor', [(i, (i + k) % size) for i in range(size)])  36.5 us
    ppermute x18, starting transfers between devices, shift(): lax.ppermute(values, 'tensor', [(i, (i + k) % size) for i in range(size)])  30.3 us
    unnamed x122, local copies, waits for them, and re-layouts  29.6 us
    ppermute x6, starting transfers between devices, gather_line(): lax.ppermute(up, 'tensor', [(i, i + 1) for i in range(k - 1, size - 1)])  18.2 us
    all_to_all x1, waiting for transfers between devices, local(): received = lax.all_to_all(sent, 'tensor', 0, 0, tiled=True)  15.9 us
    ppermute x8, waiting for transfers between devices, swap(): lax.ppermute(values, axis, [(i, i ^ bit) for i in range(lax.axis_size(axi...  15.5 us
  transfers between devices with their start and end apart: 43, of which 13 were waited for; matrix products, arithmetic and copies ran while one was open for 3% of the time, Pallas kernels for 26%

profile of v2, /device:TPU:0, one launch (start us, length us, event | category | flops | bytes accessed | tf_op | source)
XLA Modules:
  0.0 389.4 jit_solution(4576135492294693716)
XLA Ops:
  13.2 1.3 collective-permute-start.1
  14.5 5.6 %collective-permute-start = (bf16[96,1792]{1,0:T(8,128)(2,1)S(1)}, bf16[96,1792]{1,0:T(8,128)(2,1)S(1)}, u32[]{:S(2)}, u32[]{:S(2)}) collective-permute-start(bf16[96,1792]{1,0:T(8,128)(2,1)S(1)} %get-tuple-element.81), channel_id=1, source_target_pairs={{0,1},{1,2},{2,3},{4,5},{5,6},{6,7},{8,9},{9,10},{10,11},{12,13},{... | collective-permute-start | bytes 1032200 | tf_op jit(solution)/shard_map/ppermute | solution.py:626
  20.2 6.0 %collective-permute-done.1 = bf16[96,1792]{1,0:T(8,128)(2,1)S(1)} collective-permute-done((bf16[96,1792]{1,0:T(8,128)(2,1)S(1)}, bf16[96,1792]{1,0:T(8,128)(2,1)S(1)}, u32[]{:S(2)}, u32[]{:S(2)}) %collective-permute-start.1) | collective-permute-done | bytes 344096 | tf_op jit(solution)/shard_map/ppermute | solution.py:627
  26.2 1.3 collective-permute-start.2
  27.5 1.4 collective-permute-start.4
  28.9 8.3 %collective-permute-start.6 = (bf16[512,768]{1,0:T(8,128)(2,1)S(1)}, bf16[512,768]{1,0:T(8,128)(2,1)S(1)}, u32[]{:S(2)}, u32[]{:S(2)}) collective-permute-start(bf16[512,768]{1,0:T(8,128)(2,1)S(1)} %copy-done.34), channel_id=1, source_target_pairs={{0,1},{1,2},{2,3},{4,5},{5,6},{6,7},{8,9},{9,10},{10,11},{12,13},{... | collective-permute-start | bytes 2359304 | tf_op jit(solution)/shard_map/ppermute | solution.py:626
  37.2 1.3 collective-permute-start.7
  38.5 1.3 collective-permute-start.3
  41.6 22.5 %collective-permute-done.3 = bf16[96,1792]{1,0:T(8,128)(2,1)S(1)} collective-permute-done((bf16[96,1792]{1,0:T(8,128)(2,1)}, bf16[96,1792]{1,0:T(8,128)(2,1)S(1)}, u32[]{:S(2)}, u32[]{:S(2)}) %collective-permute-start.3) | collective-permute-done | bytes 344096 | tf_op jit(solution)/shard_map/ppermute | solution.py:627
  64.2 1.2 pad_maximum_fusion
  65.4 1.3 collective-permute-start.10
  66.7 1.6 collective-permute-start.8
  68.8 15.2 %collective-permute-done.10.refs_8_ = bf16[512,768]{1,0:T(8,128)(2,1)} collective-permute-done((bf16[512,768]{1,0:T(8,128)(2,1)S(1)}, bf16[512,768]{1,0:T(8,128)(2,1)}, u32[]{:S(2)}, u32[]{:S(2)}) %collective-permute-start.10) | collective-permute-done | bytes 786464 | tf_op jit(solution)/shard_map/ppermute | solution.py:627
  84.1 1.3 collective-permute-start.11
  86.1 7.9 %slot_tokens.1 = (f32[3,1,2048]{2,1,0:T(1,128)S(1)}, f32[3,1,2048]{2,1,0:T(1,128)S(1)}) custom-call(s32[6]{0:T(128)S(1)} %pad_add_fusion.refs_0_, s32[3,1,2048]{2,1,0:T(1,128)S(1)} %bitcast.22, s32[1,2048]{1,0:T(1,128)S(1)} %copy-done.47), custom_call_target="tpu_custom_call" | custom-call | flops 9200000000 | tf_op jit(solution)/shard_map/slot_tokens/pallas_call | solution.py:460
  94.0 7.9 %collective-permute-done.11.refs_9_ = bf16[512,768]{1,0:T(8,128)(2,1)S(1)} collective-permute-done((bf16[512,768]{1,0:T(8,128)(2,1)}, bf16[512,768]{1,0:T(8,128)(2,1)S(1)}, u32[]{:S(2)}, u32[]{:S(2)}) %collective-permute-start.11) | collective-permute-done | bytes 786464 | tf_op jit(solution)/shard_map/ppermute | solution.py:627
  101.9 8.2 %project.1 = (bf16[2048,768]{1,0:T(8,128)(2,1)S(1)}, bf16[3,2048,256]{2,1,0:T(8,128)(2,1)S(1)}) custom-call(s32[6]{0:T(128)S(1)} %pad_add_fusion.refs_0_, bf16[512,768]{1,0:T(8,128)(2,1)S(1)} %copy-done.34, bf16[768,768]{1,0:T(8,128)(2,1)S(1)} %copy-done.33, f32[1,768]{1,0:T(1,128)S(1)} %bitcast.20, bf16[512,768]{1,0:T(8,128)(2,1)S(1)} %collective-permute-done.6.refs_4_, ...), custom_call_target="tpu_custom_call" | custom-call | flops 6899999744 | tf_op jit(solution)/shard_map/project/pallas_call | solution.py:460
  110.1 1.6 copy-done.3
  111.8 31.3 %attend.1 = (bf16[3,2048,256]{2,1,0:T(8,128)(2,1)S(1)}, bf16[4,800,128]{2,1,0:T(8,128)(2,1)S(1)}) custom-call(s32[6]{0:T(128)S(1)} %pad_add_fusion.refs_0_, f32[3,1,2048]{2,1,0:T(1,128)S(1)} %get-tuple-element.78.refs_10_.refs_1_.refs_0_, f32[3,1,2048]{2,1,0:T(1,128)S(1)} %get-tuple-element.79.refs_2_.refs_1_, ...), custom_call_target="tpu_custom_call" | custom-call | flops 34500001792 | tf_op jit(solution)/shard_map/attend/pallas_call | solution.py:460
  144.0 6.7 %all-to-all-start = ((bf16[4,800,128]{2,1,0:T(8,128)(2,1)}), bf16[4,800,128]{2,1,0:T(8,128)(2,1)}, u32[]{:S(2)}, u32[]{:S(2)}) async-start(bf16[4,800,128]{2,1,0:T(8,128)(2,1)} %copy-done.9), calls=%async_computation | async-start | bytes 1638400 | tf_op jit(solution)/shard_map/all_to_all | solution.py:733
  151.7 15.9 %all-to-all-done.refs_4_ = bf16[4,800,128]{2,1,0:T(8,128)(2,1)} async-done(((bf16[4,800,128]{2,1,0:T(8,128)(2,1)}), bf16[4,800,128]{2,1,0:T(8,128)(2,1)}, u32[]{:S(2)}, u32[]{:S(2)}) %all-to-all-start) | async-done | bytes 819232 | tf_op jit(solution)/shard_map/all_to_all | solution.py:733
  167.6 26.9 %layer.1 = (bf16[512,768]{1,0:T(8,128)(2,1)}, f32[512,768]{1,0:T(8,128)}, bf16[512,3072]{1,0:T(8,128)(2,1)}, bf16[512,3072]{1,0:T(8,128)(2,1)}, bf16[512,768]{1,...) custom-call(s32[6]{0:T(128)} %copy-done.32, ...), custom_call_target="tpu_custom_call" | custom-call | flops 27599998976 | tf_op jit(solution)/shard_map/layer/pallas_call | solution.py:460
  194.5 1.9 copy-done.5
  196.4 1.9 copy-done.6
  198.3 1.2 copy-done.8
  202.9 9.7 %turned.1.refs_8_ = bf16[768,7168]{1,0:T(8,128)(2,1)S(1)} custom-call(bf16[512,768]{1,0:T(8,128)(2,1)S(1)} %copy-done.11, bf16[512,768]{1,0:T(8,128)(2,1)S(1)} %copy-done.12, bf16[512,768]{1,0:T(8,128)(2,1)S(1)} %copy-done.13, bf16[512,3072]{1,0:T(8,128)(2,1)S(1)} %copy-done.6, bf16[512,3072]{1,0:T(8,128)(2,1)S(1)} %copy-done.5, bf16[512,1024]{1,0:T(8,128)(2,1)S(1)} %copy-done.8), custom_call_target="tpu_custom_call" | custom-call | flops 1150000000 | tf_op jit(solution)/shard_map/turned/pallas_call | solution.py:460
  212.7 4.1 %copy-done = bf16[768,7168]{1,0:T(8,128)(2,1)} copy-done((bf16[768,7168]{1,0:T(8,128)(2,1)}, bf16[768,7168]{1,0:T(8,128)(2,1)S(1)}, u32[]{:S(2)}) %copy-start) | copy-done | bytes 11010072
  216.9 2.0 collective-permute-start.13
  218.9 1.8 collective-permute-start.14
  220.7 3.9 collective-permute-done.12
  224.6 3.4 collective-permute-done.13
  228.0 1.8 pad_maximum_fusion.1
  229.9 2.5 collective-permute-start.15
  232.4 1.9 collective-permute-start.16
  235.5 1.6 collective-permute-start.21
  237.1 1.9 copy-done.4
  239.0 3.4 flip.1.refs_3_
  242.4 4.1 %collective-permute-done.21 = f32[12,768]{1,0:T(8,128)S(1)} collective-permute-done((f32[12,768]{1,0:T(8,128)S(1)}, f32[12,768]{1,0:T(8,128)S(1)}, u32[]{:S(2)}, u32[]{:S(2)}) %collective-permute-start.21) | collective-permute-done | bytes 36896 | tf_op jit(solution)/shard_map/ppermute | solution.py:634
  246.6 2.8 collective-permute-start.25
  249.4 13.9 %attend_back.3 = (bf16[768,128]{1,0:T(8,128)(2,1)S(1)}, bf16[768,128]{1,0:T(8,128)(2,1)S(1)}, bf16[768,128]{1,0:T(8,128)(2,1)S(1)}, bf16[768,128]{1,0:T(8,128)(2...) custom-call(f32[3,1,2048]{2,1,0:T(1,128)S(1)} %get-tuple-element.78.refs_10_.refs_1_.refs_, ...), custom_call_target="tpu_custom_call" | custom-call | flops 3449999872 | tf_op jit(solution)/shard_map/attend_back/pallas_call | solution.py:460
  263.3 2.8 collective-permute-start.18
  267.2 1.5 collective-permute-start.20
  270.2 13.9 %attend_back.4 = (bf16[768,128]{1,0:T(8,128)(2,1)S(1)}, bf16[768,128]{1,0:T(8,128)(2,1)}, bf16[768,128]{1,0:T(8,128)(2,1)S(1)}, bf16[768,128]{1,0:T(8,128)(2,1)S...) custom-call(f32[3,1,2048]{2,1,0:T(1,128)S(1)} %copy-done.28, ...), custom_call_target="tpu_custom_call" | custom-call | flops 3449999872 | tf_op jit(solution)/shard_map/attend_back/pallas_call | solution.py:460
  284.9 13.9 %attend_back.5 = (bf16[768,128]{1,0:T(8,128)(2,1)S(1)}, bf16[768,128]{1,0:T(8,128)(2,1)}, bf16[768,128]{1,0:T(8,128)(2,1)}, bf16[768,128]{1,0:T(8,128)(2,1)S(1)}...) custom-call(f32[3,1,2048]{2,1,0:T(1,128)S(1)} %copy-done.29, ...), custom_call_target="tpu_custom_call" | custom-call | flops 3449999872 | tf_op jit(solution)/shard_map/attend_back/pallas_call | solution.py:460
  299.7 1.3 collective-permute-done.29
  301.2 1.7 collective-permute-start.30
  303.3 8.1 %collective-permute-done.33 = f32[15,768]{1,0:T(8,128)S(1)} collective-permute-done((f32[15,768]{1,0:T(8,128)S(1)}, f32[15,768]{1,0:T(8,128)S(1)}, u32[]{:S(2)}, u32[]{:S(2)}) %collective-permute-start.33) | collective-permute-done | bytes 46112 | tf_op jit(solution)/shard_map/ppermute | solution.py:634
  311.5 1.6 collective-permute-start.34
  313.8 1.8 collective-permute-start.23
  315.6 1.3 collective-permute-start.24
  317.9 1.4 collective-permute-start.31
  321.3 1.8 collective-permute-done.31
  323.8 2.2 fusion.23
  326.1 1.9 collective-permute-start.35
  328.6 1.8 collective-permute-start.36
  330.4 16.0 %collective-permute-done.23.refs_4_ = bf16[768,128]{1,0:T(8,128)(2,1)S(1)} collective-permute-done((bf16[768,128]{1,0:T(8,128)(2,1)S(1)}, bf16[768,128]{1,0:T(8,128)(2,1)S(1)}, u32[]{:S(2)}, u32[]{:S(2)}) %collective-permute-start.23) | collective-permute-done | bytes 196640 | tf_op jit(solution)/shard_map/ppermute | solution.py:615
  348.3 3.9 collective-permute-start.27
  352.2 3.4 collective-permute-start.28
  355.6 2.3 copy-done.1
  358.9 1.4 finish.3.refs_0_
  360.4 2.4 finish.4.refs_0_
  362.8 13.1 %collective-permute-done.27.refs_4_ = bf16[768,128]{1,0:T(8,128)(2,1)} collective-permute-done((bf16[768,128]{1,0:T(8,128)(2,1)}, bf16[768,128]{1,0:T(8,128)(2,1)}, u32[]{:S(2)}, u32[]{:S(2)}) %collective-permute-start.27) | collective-permute-done | bytes 196640 | tf_op jit(solution)/shard_map/ppermute | solution.py:615
  375.9 3.7 finish.5
  379.7 1.3 convert_add_fusion
  (205 shorter events, 29.9 us)
Async XLA Ops:
  7.2 58.2 %all-gather.4.cloned.1.call-start = ((), (), s32[]{:S(2)}) async-start(), calls=%async_computation.2 | async-start | bytes 1327104 | tf_op jit(solution)/shard_map/all_gather | solution.py:700
  12.3 16.6 %copy-start.34 = (bf16[512,768]{1,0:T(8,128)(2,1)S(1)}, bf16[512,768]{1,0:T(8,128)(2,1)}, u32[]{:S(2)}) copy-start(bf16[512,768]{1,0:T(8,128)(2,1)} %refs_1_.5) | copy-start | bytes 2359300
  13.2 13.0 %collective-permute-start.1 = (bf16[96,1792]{1,0:T(8,128)(2,1)S(1)}, bf16[96,1792]{1,0:T(8,128)(2,1)S(1)}, u32[]{:S(2)}, u32[]{:S(2)}) collective-permute-start(bf16[96,1792]{1,0:T(8,128)(2,1)S(1)} %get-tuple-element.81), channel_id=1, source_target_pairs={{1,0},{2,1},{3,2},{5,4},{6,5},{7,6},{9,8},{10,9},{11,10},{13,12},{... | collective-permute-start | bytes 1032200 | tf_op jit(solution)/shard_map/ppermute | solution.py:627
  14.5 13.0 %collective-permute-start = (bf16[96,1792]{1,0:T(8,128)(2,1)S(1)}, bf16[96,1792]{1,0:T(8,128)(2,1)S(1)}, u32[]{:S(2)}, u32[]{:S(2)}) collective-permute-start(bf16[96,1792]{1,0:T(8,128)(2,1)S(1)} %get-tuple-element.81), channel_id=1, source_target_pairs={{0,1},{1,2},{2,3},{4,5},{5,6},{6,7},{8,9},{9,10},{10,11},{12,13},{... | collective-permute-start | bytes 1032200 | tf_op jit(solution)/shard_map/ppermute | solution.py:626
  20.1 147.5 %all-gather.6.cloned.1.call-start = ((), (), s32[]{:S(2)}) async-start(), calls=%async_computation.3 | async-start | bytes 12386304 | tf_op jit(solution)/shard_map/all_gather | solution.py:690
  26.2 12.3 %collective-permute-start.2 = (bf16[96,1792]{1,0:T(8,128)(2,1)S(1)}, bf16[96,1792]{1,0:T(8,128)(2,1)}, u32[]{:S(2)}, u32[]{:S(2)}) collective-permute-start(bf16[96,1792]{1,0:T(8,128)(2,1)S(1)} %collective-permute-done.1), channel_id=1, source_target_pairs={{1,0},{2,1},{5,4},{6,5},{9,8},{10,9},{13,12},{14,13},{17,16},{18,1... | collective-permute-start | bytes 1032200 | tf_op jit(solution)/shard_map/ppermute | solution.py:627
  27.5 12.3 %collective-permute-start.4 = (bf16[96,1792]{1,0:T(8,128)(2,1)S(1)}, bf16[96,1792]{1,0:T(8,128)(2,1)}, u32[]{:S(2)}, u32[]{:S(2)}) collective-permute-start(bf16[96,1792]{1,0:T(8,128)(2,1)S(1)} %collective-permute-done), channel_id=1, source_target_pairs={{1,2},{2,3},{5,6},{6,7},{9,10},{10,11},{13,14},{14,15},{17,18},{18... | collective-permute-start | bytes 1032200 | tf_op jit(solution)/shard_map/ppermute | solution.py:626
  28.9 36.5 %collective-permute-start.6 = (bf16[512,768]{1,0:T(8,128)(2,1)S(1)}, bf16[512,768]{1,0:T(8,128)(2,1)S(1)}, u32[]{:S(2)}, u32[]{:S(2)}) collective-permute-start(bf16[512,768]{1,0:T(8,128)(2,1)S(1)} %copy-done.34), channel_id=1, source_target_pairs={{0,1},{1,2},{2,3},{4,5},{5,6},{6,7},{8,9},{9,10},{10,11},{12,13},{... | collective-permute-start | bytes 2359304 | tf_op jit(solution)/shard_map/ppermute | solution.py:626
  37.2 28.2 %collective-permute-start.7 = (bf16[512,768]{1,0:T(8,128)(2,1)S(1)}, bf16[512,768]{1,0:T(8,128)(2,1)S(1)}, u32[]{:S(2)}, u32[]{:S(2)}) collective-permute-start(bf16[512,768]{1,0:T(8,128)(2,1)S(1)} %copy-done.34), channel_id=1, source_target_pairs={{1,0},{2,1},{3,2},{5,4},{6,5},{7,6},{9,8},{10,9},{11,10},{13,12},{... | collective-permute-start | bytes 2359304 | tf_op jit(solution)/shard_map/ppermute | solution.py:627
  38.5 25.5 %collective-permute-start.3 = (bf16[96,1792]{1,0:T(8,128)(2,1)}, bf16[96,1792]{1,0:T(8,128)(2,1)S(1)}, u32[]{:S(2)}, u32[]{:S(2)}) collective-permute-start(bf16[96,1792]{1,0:T(8,128)(2,1)} %collective-permute-done.2), channel_id=1, source_target_pairs={{1,0},{5,4},{9,8},{13,12},{17,16},{21,20},{25,24},{29,28}} | collective-permute-start | bytes 1032200 | tf_op jit(solution)/shard_map/ppermute | solution.py:627
  39.8 24.3 %collective-permute-start.5 = (bf16[96,1792]{1,0:T(8,128)(2,1)}, bf16[96,1792]{1,0:T(8,128)(2,1)S(1)}, u32[]{:S(2)}, u32[]{:S(2)}) collective-permute-start(bf16[96,1792]{1,0:T(8,128)(2,1)} %collective-permute-done.4), channel_id=1, source_target_pairs={{2,3},{6,7},{10,11},{14,15},{18,19},{22,23},{26,27},{30,31}} | collective-permute-start | bytes 1032200 | tf_op jit(solution)/shard_map/ppermute | solution.py:626
  64.2 21.9 %copy-start.46 = (s32[1,3,2048]{2,0,1:T(1,128)S(1)}, s32[1,3,2048]{2,0,1:T(1,128)}, u32[]{:S(2)}) copy-start(s32[1,3,2048]{2,0,1:T(1,128)} %param.24) | copy-start | bytes 73732
  64.2 21.9 %copy-start.47 = (s32[1,2048]{1,0:T(1,128)S(1)}, s32[1,2048]{1,0:T(1,128)}, u32[]{:S(2)}) copy-start(s32[1,2048]{1,0:T(1,128)} %refs_2_.3) | copy-start | bytes 24580
  65.4 18.6 %collective-permute-start.10 = (bf16[512,768]{1,0:T(8,128)(2,1)S(1)}, bf16[512,768]{1,0:T(8,128)(2,1)}, u32[]{:S(2)}, u32[]{:S(2)}) collective-permute-start(bf16[512,768]{1,0:T(8,128)(2,1)S(1)} %collective-permute-done.7.refs_7_), channel_id=1, source_target_pairs={{1,0},{2,1},{5,4},{6,5},{9,8},{10,9},{13,12},{14,13},{17,16},{18,1... | collective-permute-start | bytes 2359304 | tf_op jit(solution)/shard_map/ppermute | solution.py:627
  66.7 18.6 %collective-permute-start.8 = (bf16[512,768]{1,0:T(8,128)(2,1)S(1)}, bf16[512,768]{1,0:T(8,128)(2,1)}, u32[]{:S(2)}, u32[]{:S(2)}) collective-permute-start(bf16[512,768]{1,0:T(8,128)(2,1)S(1)} %collective-permute-done.6.refs_4_), channel_id=1, source_target_pairs={{1,2},{2,3},{5,6},{6,7},{9,10},{10,11},{13,14},{14,15},{17,18},{18... | collective-permute-start | bytes 2359304 | tf_op jit(solution)/shard_map/ppermute | solution.py:626
  68.8 43.0 %copy-start.32 = (s32[6]{0:T(128)}, s32[6]{0:T(128)S(1)}, u32[]{:S(2)}) copy-start(s32[6]{0:T(128)S(1)} %pad_add_fusion.refs_0_) | copy-start | bytes 76
  84.1 17.8 %collective-permute-start.11 = (bf16[512,768]{1,0:T(8,128)(2,1)}, bf16[512,768]{1,0:T(8,128)(2,1)S(1)}, u32[]{:S(2)}, u32[]{:S(2)}) collective-permute-start(bf16[512,768]{1,0:T(8,128)(2,1)} %collective-permute-done.10.refs_8_), channel_id=1, source_target_pairs={{1,0},{5,4},{9,8},{13,12},{17,16},{21,20},{25,24},{29,28}} | collective-permute-start | bytes 2359304 | tf_op jit(solution)/shard_map/ppermute | solution.py:627
  85.4 16.5 %collective-permute-start.9 = (bf16[512,768]{1,0:T(8,128)(2,1)}, bf16[512,768]{1,0:T(8,128)(2,1)S(1)}, u32[]{:S(2)}, u32[]{:S(2)}) collective-permute-start(bf16[512,768]{1,0:T(8,128)(2,1)} %collective-permute-done.8.refs_5_), channel_id=1, source_target_pairs={{2,3},{6,7},{10,11},{14,15},{18,19},{22,23},{26,27},{30,31}} | collective-permute-start | bytes 2359304 | tf_op jit(solution)/shard_map/ppermute | solution.py:626
  86.1 15.8 %copy-start.33 = (bf16[768,768]{1,0:T(8,128)(2,1)S(1)}, bf16[768,768]{1,0:T(8,128)(2,1)}, u32[]{:S(2)}) copy-start(bf16[768,768]{1,0:T(8,128)(2,1)} %all-gather.4.cloned.1.call-done.refs_2_) | copy-start | bytes 3538948
  94.0 155.4 %copy-start.27 = (f32[3,1,2048]{2,1,0:T(1,128)}, f32[3,1,2048]{2,1,0:T(1,128)S(1)}, u32[]{:S(2)}) copy-start(f32[3,1,2048]{2,1,0:T(1,128)S(1)} %get-tuple-element.78.refs_10_.refs_1_.refs_0_) | copy-start | bytes 73732
  94.0 155.4 %copy-start.30 = (f32[3,1,2048]{2,1,0:T(1,128)}, f32[3,1,2048]{2,1,0:T(1,128)S(1)}, u32[]{:S(2)}) copy-start(f32[3,1,2048]{2,1,0:T(1,128)S(1)} %get-tuple-element.79.refs_2_.refs_1_) | copy-start | bytes 73732
  144.0 23.7 %all-to-all-start = ((bf16[4,800,128]{2,1,0:T(8,128)(2,1)}), bf16[4,800,128]{2,1,0:T(8,128)(2,1)}, u32[]{:S(2)}, u32[]{:S(2)}) async-start(bf16[4,800,128]{2,1,0:T(8,128)(2,1)} %copy-done.9), calls=%async_computation | async-start | bytes 1638400 | tf_op jit(solution)/shard_map/all_to_all | solution.py:733
  150.7 173.2 %reduce-scatter.2.cloned.1.call-start = ((), (), s32[]{:S(2)}) async-start(), calls=%async_computation.5 | async-start | bytes 12386304 | tf_op jit(solution)/shard_map/reduce_scatter | solution.py:742
  216.8 18.7 %copy-start.48 = (f32[12,768]{1,0:T(8,128)S(1)}, f32[12,768]{1,0:T(8,128)}, u32[]{:S(2)}) copy-start(f32[12,768]{1,0:T(8,128)} %get-tuple-element.108) | copy-start | bytes 110596
  216.8 138.8 %all-gather.8.cloned.1.call-start = ((), (), s32[]{:S(2)}) async-start(), calls=%async_computation.4 | async-start | bytes 5308416 | tf_op jit(solution)/shard_map/all_gather | solution.py:690
  216.8 7.8 %collective-permute-start.12 = (bf16[96,768]{1,0:T(8,128)(2,1)}, bf16[96,768]{1,0:T(8,128)(2,1)S(1)}, u32[]{:S(2)}, u32[]{:S(2)}) collective-permute-start(bf16[96,768]{1,0:T(8,128)(2,1)} %get-tuple-element.91), channel_id=1, source_target_pairs={{0,1},{1,2},{2,3},{3,0},{4,5},{5,6},{6,7},{7,4},{8,9},{9,10},{10,1... | collective-permute-start | bytes 442376 | tf_op jit(solution)/shard_map/ppermute | solution.py:615
  216.9 11.1 %collective-permute-start.13 = (bf16[96,768]{1,0:T(8,128)(2,1)}, bf16[96,768]{1,0:T(8,128)(2,1)S(1)}, u32[]{:S(2)}, u32[]{:S(2)}) collective-permute-start(bf16[96,768]{1,0:T(8,128)(2,1)} %get-tuple-element.91), channel_id=1, source_target_pairs={{0,2},{1,3},{2,0},{3,1},{4,6},{5,7},{6,4},{7,5},{8,10},{9,11},{10,... | collective-permute-start | bytes 442376 | tf_op jit(solution)/shard_map/ppermute | solution.py:615
  218.9 9.1 %collective-permute-start.14 = (bf16[96,768]{1,0:T(8,128)(2,1)}, bf16[96,768]{1,0:T(8,128)(2,1)S(1)}, u32[]{:S(2)}, u32[]{:S(2)}) collective-permute-start(bf16[96,768]{1,0:T(8,128)(2,1)} %get-tuple-element.91), channel_id=1, source_target_pairs={{0,3},{1,0},{2,1},{3,2},{4,7},{5,4},{6,5},{7,6},{8,11},{9,8},{10,9... | collective-permute-start | bytes 442376 | tf_op jit(solution)/shard_map/ppermute | solution.py:615
  229.9 16.7 %collective-permute-start.15 = (bf16[768,128]{1,0:T(8,128)(2,1)}, bf16[768,128]{1,0:T(8,128)(2,1)S(1)}, u32[]{:S(2)}, u32[]{:S(2)}) collective-permute-start(bf16[768,128]{1,0:T(8,128)(2,1)} %get-tuple-element.95), channel_id=1, source_target_pairs={{0,1},{1,2},{2,3},{3,0},{4,5},{5,6},{6,7},{7,4},{8,9},{9,10},{10,1... | collective-permute-start | bytes 589832 | tf_op jit(solution)/shard_map/ppermute | solution.py:615
  232.4 14.2 %collective-permute-start.16 = (bf16[768,128]{1,0:T(8,128)(2,1)}, bf16[768,128]{1,0:T(8,128)(2,1)S(1)}, u32[]{:S(2)}, u32[]{:S(2)}) collective-permute-start(bf16[768,128]{1,0:T(8,128)(2,1)} %get-tuple-element.96), channel_id=1, source_target_pairs={{0,2},{1,3},{2,0},{3,1},{4,6},{5,7},{6,4},{7,5},{8,10},{9,11},{10,... | collective-permute-start | bytes 589832 | tf_op jit(solution)/shard_map/ppermute | solution.py:615
  234.3 12.3 %collective-permute-start.17 = (bf16[768,128]{1,0:T(8,128)(2,1)}, bf16[768,128]{1,0:T(8,128)(2,1)S(1)}, u32[]{:S(2)}, u32[]{:S(2)}) collective-permute-start(bf16[768,128]{1,0:T(8,128)(2,1)} %get-tuple-element.97), channel_id=1, source_target_pairs={{0,3},{1,0},{2,1},{3,2},{4,7},{5,4},{6,5},{7,6},{8,11},{9,8},{10,9... | collective-permute-start | bytes 589832 | tf_op jit(solution)/shard_map/ppermute | solution.py:615
  235.5 11.0 %collective-permute-start.21 = (f32[12,768]{1,0:T(8,128)S(1)}, f32[12,768]{1,0:T(8,128)S(1)}, u32[]{:S(2)}, u32[]{:S(2)}) collective-permute-start(f32[12,768]{1,0:T(8,128)S(1)} %copy-done.48), channel_id=1, source_target_pairs={{0,1},{1,0},{2,3},{3,2},{4,5},{5,4},{6,7},{7,6},{8,9},{9,8},{10,11... | collective-permute-start | bytes 110600 | tf_op jit(solution)/shard_map/ppermute | solution.py:634
  239.0 10.4 %copy-start.10 = (bf16[768,128]{1,0:T(8,128)(2,1)S(1)}, bf16[768,128]{1,0:T(8,128)(2,1)}, u32[]{:S(2)}) copy-start(bf16[768,128]{1,0:T(8,128)(2,1)} %get-tuple-element.118.refs_4_) | copy-start | bytes 589828
  246.6 38.2 %collective-permute-start.25 = (f32[12,768]{1,0:T(8,128)S(1)}, f32[12,768]{1,0:T(8,128)S(1)}, u32[]{:S(2)}, u32[]{:S(2)}) collective-permute-start(f32[12,768]{1,0:T(8,128)S(1)} %add.96), channel_id=1, source_target_pairs={{0,2},{1,3},{2,0},{3,1},{4,6},{5,7},{6,4},{7,5},{8,10},{9,11},{10,... | collective-permute-start | bytes 110600 | tf_op jit(solution)/shard_map/ppermute | solution.py:634
  263.3 21.5 %collective-permute-start.18 = (bf16[768,128]{1,0:T(8,128)(2,1)S(1)}, bf16[768,128]{1,0:T(8,128)(2,1)S(1)}, u32[]{:S(2)}, u32[]{:S(2)}) collective-permute-start(bf16[768,128]{1,0:T(8,128)(2,1)S(1)} %get-tuple-element.105), channel_id=1, source_target_pairs={{0,1},{1,2},{2,3},{3,0},{4,5},{5,6},{6,7},{7,4},{8,9},{9,10},{10,1... | collective-permute-start | bytes 589832 | tf_op jit(solution)/shard_map/ppermute | solution.py:615
  266.1 18.7 %collective-permute-start.19 = (bf16[768,128]{1,0:T(8,128)(2,1)S(1)}, bf16[768,128]{1,0:T(8,128)(2,1)S(1)}, u32[]{:S(2)}, u32[]{:S(2)}) collective-permute-start(bf16[768,128]{1,0:T(8,128)(2,1)S(1)} %get-tuple-element.106), channel_id=1, source_target_pairs={{0,2},{1,3},{2,0},{3,1},{4,6},{5,7},{6,4},{7,5},{8,10},{9,11},{10,... | collective-permute-start | bytes 589832 | tf_op jit(solution)/shard_map/ppermute | solution.py:615
  267.2 17.6 %collective-permute-start.20 = (bf16[768,128]{1,0:T(8,128)(2,1)S(1)}, bf16[768,128]{1,0:T(8,128)(2,1)S(1)}, u32[]{:S(2)}, u32[]{:S(2)}) collective-permute-start(bf16[768,128]{1,0:T(8,128)(2,1)S(1)} %get-tuple-element.107), channel_id=1, source_target_pairs={{0,3},{1,0},{2,1},{3,2},{4,7},{5,4},{6,5},{7,6},{8,11},{9,8},{10,9... | collective-permute-start | bytes 589832 | tf_op jit(solution)/shard_map/ppermute | solution.py:615
  270.2 14.7 %copy-start.29 = (f32[3,1,2048]{2,1,0:T(1,128)S(1)}, f32[3,1,2048]{2,1,0:T(1,128)}, u32[]{:S(2)}) copy-start(f32[3,1,2048]{2,1,0:T(1,128)} %copy-done.27) | copy-start | bytes 73732
  284.8 14.0 %copy-start.18 = (bf16[768,128]{1,0:T(8,128)(2,1)}, bf16[768,128]{1,0:T(8,128)(2,1)S(1)}, u32[]{:S(2)}) copy-start(bf16[768,128]{1,0:T(8,128)(2,1)S(1)} %get-tuple-element.113.refs_2_) | copy-start | bytes 589828
  284.8 14.0 %copy-start.35 = (bf16[768,128]{1,0:T(8,128)(2,1)}, bf16[768,128]{1,0:T(8,128)(2,1)S(1)}, u32[]{:S(2)}) copy-start(bf16[768,128]{1,0:T(8,128)(2,1)S(1)} %get-tuple-element.115) | copy-start | bytes 589828
  284.8 14.0 %copy-start.14 = (bf16[768,128]{1,0:T(8,128)(2,1)}, bf16[768,128]{1,0:T(8,128)(2,1)S(1)}, u32[]{:S(2)}) copy-start(bf16[768,128]{1,0:T(8,128)(2,1)S(1)} %collective-permute-done.19.refs_4_.refs_9_) | copy-start | bytes 589828
  284.9 14.0 %copy-start.16 = (bf16[768,128]{1,0:T(8,128)(2,1)}, bf16[768,128]{1,0:T(8,128)(2,1)S(1)}, u32[]{:S(2)}) copy-start(bf16[768,128]{1,0:T(8,128)(2,1)S(1)} %collective-permute-done.20.refs_5_.refs_10_) | copy-start | bytes 589828
  298.9 2.1 collective-permute-start.29
  299.0 14.1 %copy-start.39 = (bf16[768,128]{1,0:T(8,128)(2,1)S(1)}, bf16[768,128]{1,0:T(8,128)(2,1)}, u32[]{:S(2)}) copy-start(bf16[768,128]{1,0:T(8,128)(2,1)} %copy-done.38) | copy-start | bytes 589828
  299.1 14.8 %copy-start.36 = (bf16[768,128]{1,0:T(8,128)(2,1)S(1)}, bf16[768,128]{1,0:T(8,128)(2,1)}, u32[]{:S(2)}) copy-start(bf16[768,128]{1,0:T(8,128)(2,1)} %copy-done.35) | copy-start | bytes 589828
  299.1 3.8 collective-permute-start.32
  301.2 16.7 %collective-permute-start.30 = (bf16[192,768]{1,0:T(8,128)(2,1)S(1)}, bf16[192,768]{1,0:T(8,128)(2,1)S(1)}, u32[]{:S(2)}, u32[]{:S(2)}) collective-permute-start(bf16[192,768]{1,0:T(8,128)(2,1)S(1)} %get-tuple-element.167), channel_id=1, source_target_pairs={{0,8},{8,0},{16,24},{24,16},{1,9},{9,1},{17,25},{25,17},{2,10},{10... | collective-permute-start | bytes 884744 | tf_op jit(solution)/shard_map/ppermute | solution.py:634
  302.9 8.6 %collective-permute-start.33 = (f32[15,768]{1,0:T(8,128)S(1)}, f32[15,768]{1,0:T(8,128)S(1)}, u32[]{:S(2)}, u32[]{:S(2)}) collective-permute-start(f32[15,768]{1,0:T(8,128)S(1)} %fusion.25), channel_id=1, source_target_pairs={{0,8},{8,0},{16,24},{24,16},{1,9},{9,1},{17,25},{25,17},{2,10},{10... | collective-permute-start | bytes 138248 | tf_op jit(solution)/shard_map/ppermute | solution.py:634
  311.5 5.5 %collective-permute-start.34 = (f32[15,768]{1,0:T(8,128)S(1)}, f32[15,768]{1,0:T(8,128)S(1)}, u32[]{:S(2)}, u32[]{:S(2)}) collective-permute-start(f32[15,768]{1,0:T(8,128)S(1)} %add.104), channel_id=1, source_target_pairs={{0,16},{8,24},{16,0},{24,8},{1,17},{9,25},{17,1},{25,9},{2,18},{10... | collective-permute-start | bytes 138248 | tf_op jit(solution)/shard_map/ppermute | solution.py:634
  313.1 14.8 %collective-permute-start.22 = (bf16[768,128]{1,0:T(8,128)(2,1)S(1)}, bf16[768,128]{1,0:T(8,128)(2,1)S(1)}, u32[]{:S(2)}, u32[]{:S(2)}) collective-permute-start(bf16[768,128]{1,0:T(8,128)(2,1)S(1)} %copy-done.39), channel_id=1, source_target_pairs={{0,1},{1,2},{2,3},{3,0},{4,5},{5,6},{6,7},{7,4},{8,9},{9,10},{10,1... | collective-permute-start | bytes 589832 | tf_op jit(solution)/shard_map/ppermute | solution.py:615
  313.8 32.6 %collective-permute-start.23 = (bf16[768,128]{1,0:T(8,128)(2,1)S(1)}, bf16[768,128]{1,0:T(8,128)(2,1)S(1)}, u32[]{:S(2)}, u32[]{:S(2)}) collective-permute-start(bf16[768,128]{1,0:T(8,128)(2,1)S(1)} %copy-done.36), channel_id=1, source_target_pairs={{0,2},{1,3},{2,0},{3,1},{4,6},{5,7},{6,4},{7,5},{8,10},{9,11},{10,... | collective-permute-start | bytes 589832 | tf_op jit(solution)/shard_map/ppermute | solution.py:615
  315.6 32.7 %collective-permute-start.24 = (bf16[768,128]{1,0:T(8,128)(2,1)}, bf16[768,128]{1,0:T(8,128)(2,1)}, u32[]{:S(2)}, u32[]{:S(2)}) collective-permute-start(bf16[768,128]{1,0:T(8,128)(2,1)} %get-tuple-element.116), channel_id=1, source_target_pairs={{0,3},{1,0},{2,1},{3,2},{4,7},{5,4},{6,5},{7,6},{8,11},{9,8},{10,9... | collective-permute-start | bytes 589832 | tf_op jit(solution)/shard_map/ppermute | solution.py:615
  316.9 35.2 %collective-permute-start.26 = (bf16[768,128]{1,0:T(8,128)(2,1)}, bf16[768,128]{1,0:T(8,128)(2,1)}, u32[]{:S(2)}, u32[]{:S(2)}) collective-permute-start(bf16[768,128]{1,0:T(8,128)(2,1)} %copy-done.37), channel_id=1, source_target_pairs={{0,1},{1,2},{2,3},{3,0},{4,5},{5,6},{6,7},{7,4},{8,9},{9,10},{10,1... | collective-permute-start | bytes 589832 | tf_op jit(solution)/shard_map/ppermute | solution.py:615
  317.9 5.2 %collective-permute-start.31 = (bf16[96,768]{1,0:T(8,128)(2,1)S(1)}, bf16[96,768]{1,0:T(8,128)(2,1)S(1)}, u32[]{:S(2)}, u32[]{:S(2)}) collective-permute-start(bf16[96,768]{1,0:T(8,128)(2,1)S(1)} %add_convert_fusion.3), channel_id=1, source_target_pairs={{0,16},{8,24},{16,0},{24,8},{1,17},{9,25},{17,1},{25,9},{2,18},{10... | collective-permute-start | bytes 442376 | tf_op jit(solution)/shard_map/ppermute | solution.py:634
  323.8 23.3 %copy-start.26 = (bf16[96,768]{1,0:T(8,128)(2,1)S(1)}, bf16[96,768]{1,0:T(8,128)(2,1)}, u32[]{:S(2)}) copy-start(bf16[96,768]{1,0:T(8,128)(2,1)} %add_convert_fusion.2.refs_0_) | copy-start | bytes 442372
  326.1 53.5 %collective-permute-start.35 = (bf16[96,1792]{1,0:T(8,128)(2,1)}, bf16[96,1792]{1,0:T(8,128)(2,1)}, u32[]{:S(2)}, u32[]{:S(2)}) collective-permute-start(bf16[96,1792]{1,0:T(8,128)(2,1)} %get-tuple-element.163), channel_id=1, source_target_pairs={{0,1},{1,2},{2,3},{3,0},{4,5},{5,6},{6,7},{7,4},{8,9},{9,10},{10,1... | collective-permute-start | bytes 1032200 | tf_op jit(solution)/shard_map/ppermute | solution.py:615
  328.6 51.0 %collective-permute-start.36 = (bf16[96,1792]{1,0:T(8,128)(2,1)}, bf16[96,1792]{1,0:T(8,128)(2,1)}, u32[]{:S(2)}, u32[]{:S(2)}) collective-permute-start(bf16[96,1792]{1,0:T(8,128)(2,1)} %get-tuple-element.165), channel_id=1, source_target_pairs={{0,2},{1,3},{2,0},{3,1},{4,6},{5,7},{6,4},{7,5},{8,10},{9,11},{10,... | collective-permute-start | bytes 1032200 | tf_op jit(solution)/shard_map/ppermute | solution.py:615
  347.2 8.4 %copy-start.2 = (bf16[96,7168]{1,0:T(8,128)(2,1)S(1)}, bf16[96,7168]{1,0:T(8,128)(2,1)}, u32[]{:S(2)}) copy-start(bf16[96,7168]{1,0:T(8,128)(2,1)} %reduce-scatter.2.cloned.1.call-done.refs_6_) | copy-start | bytes 4128772
  347.2 8.4 %copy-start.7 = (f32[512,768]{1,0:T(8,128)S(1)}, f32[512,768]{1,0:T(8,128)}, u32[]{:S(2)}) copy-start(f32[512,768]{1,0:T(8,128)} %get-tuple-element.90.refs_0_) | copy-start | bytes 4718596
  347.2 8.4 %copy-start.15 = (bf16[768,128]{1,0:T(8,128)(2,1)S(1)}, bf16[768,128]{1,0:T(8,128)(2,1)}, u32[]{:S(2)}) copy-start(bf16[768,128]{1,0:T(8,128)(2,1)} %copy-done.14) | copy-start | bytes 589828
  347.2 32.5 %collective-permute-start.37 = (bf16[96,1792]{1,0:T(8,128)(2,1)}, bf16[96,1792]{1,0:T(8,128)(2,1)}, u32[]{:S(2)}, u32[]{:S(2)}) collective-permute-start(bf16[96,1792]{1,0:T(8,128)(2,1)} %get-tuple-element.164), channel_id=1, source_target_pairs={{0,3},{1,0},{2,1},{3,2},{4,7},{5,4},{6,5},{7,6},{8,11},{9,8},{10,9... | collective-permute-start | bytes 1032200 | tf_op jit(solution)/shard_map/ppermute | solution.py:615
  348.3 27.6 %collective-permute-start.27 = (bf16[768,128]{1,0:T(8,128)(2,1)}, bf16[768,128]{1,0:T(8,128)(2,1)}, u32[]{:S(2)}, u32[]{:S(2)}) collective-permute-start(bf16[768,128]{1,0:T(8,128)(2,1)} %get-tuple-element.124), channel_id=1, source_target_pairs={{0,2},{1,3},{2,0},{3,1},{4,6},{5,7},{6,4},{7,5},{8,10},{9,11},{10,... | collective-permute-start | bytes 589832 | tf_op jit(solution)/shard_map/ppermute | solution.py:615
  352.2 23.7 %collective-permute-start.28 = (bf16[768,128]{1,0:T(8,128)(2,1)}, bf16[768,128]{1,0:T(8,128)(2,1)}, u32[]{:S(2)}, u32[]{:S(2)}) collective-permute-start(bf16[768,128]{1,0:T(8,128)(2,1)} %get-tuple-element.125), channel_id=1, source_target_pairs={{0,3},{1,0},{2,1},{3,2},{4,7},{5,4},{6,5},{7,6},{8,11},{9,8},{10,9... | collective-permute-start | bytes 589832 | tf_op jit(solution)/shard_map/ppermute | solution.py:615
  360.4 15.6 %copy-start.21 = (bf16[768,128]{1,0:T(8,128)(2,1)S(1)}, bf16[768,128]{1,0:T(8,128)(2,1)}, u32[]{:S(2)}) copy-start(bf16[768,128]{1,0:T(8,128)(2,1)} %copy-done.20) | copy-start | bytes 589828
  (38 other events, 97.3 us)
Sparse Core Ops, SparseCore 0:
  20.3 24.7 all-gather.3
  65.5 66.0 all-gather.5
  216.9 83.2 reduce-scatter.1
  301.9 40.2 all-gather.7
